TPU v7x, 512 devices: a whole 4x8x8 slice. The times are simulated.
512 devices in a mesh: dp: 16 (over x_lo, y), tensor: 32 (over z, x_hi, core).
Axes of the slice: x: 4 (x_hi: 2, x_lo: 2; x = x_hi * 2 + x_lo), y: 8, z: 8, core: 2. Of those that a mesh axis runs over, the one named last changes fastest.
Arguments:
- tokens_in: bfloat16 [8192, 128, 128], P('dp', 'tensor'), may hold values from -6 to 6
- right_one: bfloat16 [128, 128, 128], P('tensor'), may hold values from -0.5 to 0.5
- left_one: bfloat16 [128, 128, 128], P('tensor'), may hold values from -0.5 to 0.5
- right_two: bfloat16 [128, 128, 128], P('tensor'), may hold values from -0.5 to 0.5
- left_two: bfloat16 [128, 128, 128], P('tensor'), may hold values from -0.5 to 0.5
- out_grad: bfloat16 [8192, 128, 128], P('dp', 'tensor'), may hold values from -6 to 6
Outputs:
- layer_out: bfloat16 [8192, 128, 128], P('dp', 'tensor')
- input_grad: bfloat16 [8192, 128, 128], P('dp', 'tensor')
- grad_right_one: float32 [128, 128, 128], P('tensor', 'dp')
- grad_left_one: float32 [128, 128, 128], P('tensor', 'dp')
- grad_right_two: float32 [128, 128, 128], P('tensor', 'dp')
- grad_left_two: float32 [128, 128, 128], P('tensor', 'dp')
All inputs are finite; a program needn't handle non-finite values.
Results may differ from a plain program's by a relative error of at most 0.0067.
Values may be sent and summed in bfloat16 or wider, within the bound.
No kernel may reach another device: no remote copies, remote signals or barrier semaphores. Data moves between devices by JAX's collectives and lax.ppermute only.
A program may use at most 64 MiB of HBM per device.

v0:
```python
import math

import jax
import jax.numpy as jnp
from jax import lax
from jax.sharding import PartitionSpec as P


def split_up(x, dim, size):
    before, after = (x.shape[:dim], x.shape[dim + 1 :])
    return jnp.moveaxis(x.reshape(*before, size, -1, *after), dim, 0)


def sent_and_summed(x, axis, dim):
    size = lax.axis_size(axis)
    pieces = lax.all_to_all(split_up(x, dim, size), axis, 0, 0, tiled=True)
    return jnp.sum(pieces, axis=0)


def in_one_piece(arrays, axis, dim, along):
    ends, at = ([], 0)
    for a in arrays[:-1]:
        at += a.shape[along]
        ends.append(at)
    both = jnp.concatenate(arrays, axis=along)
    return tuple(jnp.split(sent_and_summed(both, axis, dim), ends, axis=along))


def gelu_value(z):
    return 0.5 * z * (1.0 + lax.erf(z / math.sqrt(2.0)))


def gelu_slope(z):
    return 0.5 * (1.0 + lax.erf(z / math.sqrt(2.0))) + z * jnp.exp(-0.5 * z * z) / math.sqrt(
        2.0 * math.pi
    )


def forward_swap(values, apply_fn):
    return apply_fn(lax.all_to_all(values, "tensor", split_axis=2, concat_axis=1, tiled=True))


def backward_swap(values):
    return lax.all_to_all(values, "tensor", split_axis=1, concat_axis=2, tiled=True)


def on_device(tokens_in, right_one, left_one, right_two, left_two, out_grad):
    bf = jnp.bfloat16
    f32 = jnp.float32
    u1 = jnp.einsum("tbi,bio->tbo", tokens_in, right_one, preferred_element_type=f32).astype(bf)

    def first_left(received):
        return (
            received,
            jnp.einsum("tbj,jbk->tjk", received, left_one, preferred_element_type=f32).astype(bf),
        )

    v1, a1 = forward_swap(u1, first_left)

    def second_right(received):
        hidden = gelu_value(received.astype(f32)).astype(bf)
        return (
            received,
            hidden,
            jnp.einsum("tjk,kjm->tkm", hidden, right_two, preferred_element_type=f32).astype(bf),
        )

    z1, hidden, u2 = forward_swap(a1, second_right)

    def second_left(received):
        return (
            received,
            jnp.einsum("tkm,mkn->tmn", received, left_two, preferred_element_type=f32).astype(bf),
        )

    v2, w2 = forward_swap(u2, second_left)

    def keep_same(received):
        return received

    mixed = forward_swap(w2, keep_same)
    layer_out = (tokens_in.astype(f32) + jnp.swapaxes(mixed, 1, 2).astype(f32)).astype(bf)

    def grad_left(received):
        return (
            received,
            jnp.einsum("tnm,mkn->tkm", received, left_two, preferred_element_type=f32).astype(bf),
        )

    dw_two, dv2 = forward_swap(out_grad, grad_left)
    gl2 = jnp.einsum("tkm,tnm->mkn", v2, dw_two, preferred_element_type=f32)
    du2 = backward_swap(dv2)
    gr2 = jnp.einsum("tjk,tkm->kjm", hidden, du2, preferred_element_type=f32)
    dh = jnp.einsum("tkm,kjm->tjk", du2, right_two, preferred_element_type=f32)
    dz1 = (dh * gelu_slope(z1.astype(f32))).astype(bf)
    da1 = backward_swap(dz1)
    gl1 = jnp.einsum("tbj,tjk->jbk", v1, da1, preferred_element_type=f32)
    dv1 = jnp.einsum("tjk,jbk->tbj", da1, left_one, preferred_element_type=f32).astype(bf)
    du1 = backward_swap(dv1)
    gr1 = jnp.einsum("tbi,tbo->bio", tokens_in, du1, preferred_element_type=f32)
    input_grad = (
        out_grad.astype(f32)
        + jnp.einsum("tbo,bio->tbi", du1, right_one, preferred_element_type=f32)
    ).astype(bf)
    gr1, gl1, gr2, gl2 = in_one_piece((gr1, gl1, gr2, gl2), "dp", 1, 0)
    return (layer_out, input_grad, gr1, gl1, gr2, gl2)


def solution(mesh):
    placed = (
        P("dp", "tensor", None),
        P("tensor", None, None),
        P("tensor", None, None),
        P("tensor", None, None),
        P("tensor", None, None),
        P("dp", "tensor", None),
    )
    return jax.shard_map(
        on_device,
        mesh=mesh,
        in_specs=placed,
        out_specs=(
            P("dp", "tensor", None),
            P("dp", "tensor", None),
            P("tensor", "dp", None),
            P("tensor", "dp", None),
            P("tensor", "dp", None),
            P("tensor", "dp", None),
        ),
        check_vma=False,
    )
```

profile of v0, /device:TPU:12, one launch (start us, length us, event | category | flops | bytes accessed | tf_op | source)
XLA Modules:
  0.0 236.5 jit_solution(6176939641022096632)
XLA Ops:
  0.7 1.4 copy.142
  2.0 0.3 fusion.4
  2.4 1.2 copy.113
  3.6 13.6 %all-to-all-start = ((bf16[512,4,128]{0,1,2:T(4,128)(2,1)}), bf16[512,4,128]{0,1,2:T(4,128)(2,1)S(1)}, u32[]{:S(2)}, u32[]{:S(2)}) async-start(bf16[512,4,128]{0,1,2:T(4,128)(2,1)} %copy.113), calls=%async_computation | async-start | bytes 1048576 | tf_op jit(solution)/shard_map/all_to_all | solution.py:40
  17.2 1.2 copy.126
  18.3 16.5 %all-to-all-done = bf16[512,4,128]{0,1,2:T(4,128)(2,1)S(1)} async-done(((bf16[512,4,128]{0,1,2:T(4,128)(2,1)}), bf16[512,4,128]{0,1,2:T(4,128)(2,1)S(1)}, u32[]{:S(2)}, u32[]{:S(2)}) %all-to-all-start) | async-done | bytes 524320 | tf_op jit(solution)/shard_map/all_to_all | solution.py:40
  34.8 5.0 %all-to-all-start.4 = ((bf16[512,4,128]{0,1,2:T(4,128)(2,1)}), bf16[512,4,128]{0,1,2:T(4,128)(2,1)S(1)}, u32[]{:S(2)}, u32[]{:S(2)}) async-start(bf16[512,4,128]{0,1,2:T(4,128)(2,1)} %copy.126), calls=%async_computation.4 | async-start | bytes 1048576 | tf_op jit(solution)/shard_map/all_to_all | solution.py:40
  39.8 0.2 copy.114
  40.1 0.6 copy-done.6
  40.7 0.3 fusion.5
  41.1 1.2 copy.116
  42.3 15.2 %all-to-all-done.4 = bf16[512,4,128]{0,1,2:T(4,128)(2,1)S(1)} async-done(((bf16[512,4,128]{0,1,2:T(4,128)(2,1)}), bf16[512,4,128]{0,1,2:T(4,128)(2,1)S(1)}, u32[]{:S(2)}, u32[]{:S(2)}) %all-to-all-start.4) | async-done | bytes 524320 | tf_op jit(solution)/shard_map/all_to_all | solution.py:40
  57.5 5.0 %all-to-all-start.1 = ((bf16[512,4,128]{0,1,2:T(4,128)(2,1)}), bf16[512,4,128]{0,1,2:T(4,128)(2,1)S(1)}, u32[]{:S(2)}, u32[]{:S(2)}) async-start(bf16[512,4,128]{0,1,2:T(4,128)(2,1)} %copy.116), calls=%async_computation.1 | async-start | bytes 1048576 | tf_op jit(solution)/shard_map/all_to_all | solution.py:40
  62.5 0.2 copy.127
  62.8 0.4 copy.128
  63.2 0.5 copy-done.7
  63.7 0.3 fusion.8
  64.0 1.2 copy.129
  65.2 15.0 %all-to-all-done.1 = bf16[512,4,128]{0,1,2:T(4,128)(2,1)S(1)} async-done(((bf16[512,4,128]{0,1,2:T(4,128)(2,1)}), bf16[512,4,128]{0,1,2:T(4,128)(2,1)S(1)}, u32[]{:S(2)}, u32[]{:S(2)}) %all-to-all-start.1) | async-done | bytes 524320 | tf_op jit(solution)/shard_map/all_to_all | solution.py:40
  80.2 5.0 %all-to-all-start.5 = ((bf16[512,128,4]{0,2,1:T(4,128)(2,1)}), bf16[512,128,4]{0,2,1:T(4,128)(2,1)}, u32[]{:S(2)}, u32[]{:S(2)}) async-start(bf16[512,128,4]{0,2,1:T(4,128)(2,1)} %copy.129), calls=%async_computation.5 | async-start | bytes 1048576 | tf_op jit(solution)/shard_map/all_to_all | solution.py:44
  85.4 1.4 copy.117
  86.8 1.6 copy.118
  88.4 14.5 %all-to-all-done.5 = bf16[512,128,4]{0,2,1:T(4,128)(2,1)} async-done(((bf16[512,128,4]{0,2,1:T(4,128)(2,1)}), bf16[512,128,4]{0,2,1:T(4,128)(2,1)}, u32[]{:S(2)}, u32[]{:S(2)}) %all-to-all-start.5) | async-done | bytes 524320 | tf_op jit(solution)/shard_map/all_to_all | solution.py:44
  103.0 2.1 copy.130
  105.1 1.5 copy.131
  106.5 1.3 fusion.2
  107.9 2.2 copy.135
  110.1 5.1 %all-to-all-start.6 = ((bf16[512,128,4]{0,2,1:T(4,128)(2,1)}), bf16[512,128,4]{0,2,1:T(4,128)(2,1)}, u32[]{:S(2)}, u32[]{:S(2)}) async-start(bf16[512,128,4]{0,2,1:T(4,128)(2,1)} %copy.135), calls=%async_computation.6 | async-start | bytes 1048576 | tf_op jit(solution)/shard_map/all_to_all | solution.py:44
  115.2 0.2 multiply_convert_fusion
  115.4 0.3 fusion.6
  115.7 1.2 copy.120
  116.9 16.0 %all-to-all-done.6 = bf16[512,128,4]{0,2,1:T(4,128)(2,1)} async-done(((bf16[512,128,4]{0,2,1:T(4,128)(2,1)}), bf16[512,128,4]{0,2,1:T(4,128)(2,1)}, u32[]{:S(2)}, u32[]{:S(2)}) %all-to-all-start.6) | async-done | bytes 524320 | tf_op jit(solution)/shard_map/all_to_all | solution.py:44
  132.9 5.0 %all-to-all-start.2 = ((bf16[512,4,128]{0,1,2:T(4,128)(2,1)}), bf16[512,4,128]{0,1,2:T(4,128)(2,1)S(1)}, u32[]{:S(2)}, u32[]{:S(2)}) async-start(bf16[512,4,128]{0,1,2:T(4,128)(2,1)} %copy.120), calls=%async_computation.2 | async-start | bytes 1048576 | tf_op jit(solution)/shard_map/all_to_all | solution.py:40
  137.9 2.1 copy.136
  140.0 1.5 copy.137
  141.4 1.1 fusion.9
  142.5 2.3 copy.138
  144.8 10.8 %all-to-all-done.2 = bf16[512,4,128]{0,1,2:T(4,128)(2,1)S(1)} async-done(((bf16[512,4,128]{0,1,2:T(4,128)(2,1)}), bf16[512,4,128]{0,1,2:T(4,128)(2,1)S(1)}, u32[]{:S(2)}, u32[]{:S(2)}) %all-to-all-start.2) | async-done | bytes 524320 | tf_op jit(solution)/shard_map/all_to_all | solution.py:40
  155.6 0.8 copy-done.5
  156.3 5.1 %all-to-all-start.7 = ((bf16[512,128,4]{0,2,1:T(4,128)(2,1)}), bf16[512,128,4]{0,2,1:T(4,128)(2,1)}, u32[]{:S(2)}, u32[]{:S(2)}) async-start(bf16[512,128,4]{0,2,1:T(4,128)(2,1)} %copy.138), calls=%async_computation.7 | async-start | bytes 1048576 | tf_op jit(solution)/shard_map/all_to_all | solution.py:44
  161.4 1.3 copy.121
  162.7 1.1 fusion.7
  163.9 2.2 copy.123
  166.1 13.0 %all-to-all-done.7 = bf16[512,128,4]{0,2,1:T(4,128)(2,1)} async-done(((bf16[512,128,4]{0,2,1:T(4,128)(2,1)}), bf16[512,128,4]{0,2,1:T(4,128)(2,1)}, u32[]{:S(2)}, u32[]{:S(2)}) %all-to-all-start.7) | async-done | bytes 524320 | tf_op jit(solution)/shard_map/all_to_all | solution.py:44
  179.1 5.0 %all-to-all-start.3 = ((bf16[512,4,128]{0,1,2:T(4,128)(2,1)}), bf16[512,4,128]{0,1,2:T(4,128)(2,1)}, u32[]{:S(2)}, u32[]{:S(2)}) async-start(bf16[512,4,128]{0,1,2:T(4,128)(2,1)} %copy.123), calls=%async_computation.3 | async-start | bytes 1048576 | tf_op jit(solution)/shard_map/all_to_all | solution.py:40
  184.2 1.4 fusion.22
  185.6 0.3 fusion.19
  185.9 0.3 fusion.16
  186.2 1.3 copy.139
  187.5 0.4 copy.140
  187.9 0.3 convolution_bitcast_fusion.2
  188.2 1.1 copy_bitcast_fusion
  189.3 12.6 %all-to-all-done.3 = bf16[512,4,128]{0,1,2:T(4,128)(2,1)} async-done(((bf16[512,4,128]{0,1,2:T(4,128)(2,1)}), bf16[512,4,128]{0,1,2:T(4,128)(2,1)}, u32[]{:S(2)}, u32[]{:S(2)}) %all-to-all-start.3) | async-done | bytes 524320 | tf_op jit(solution)/shard_map/all_to_all | solution.py:40
  201.9 8.2 %all-to-all-start.8 = ((f32[16,16,8,128]{3,2,1,0:T(8,128)}), f32[16,16,8,128]{3,2,1,0:T(8,128)S(1)}, u32[]{:S(2)}, u32[]{:S(2)}) async-start(f32[16,16,8,128]{3,2,1,0:T(8,128)} %copy_bitcast_fusion), calls=%async_computation.8 | async-start | bytes 2097152 | tf_op jit(solution)/shard_map/all_to_all | solution.py:16
  210.1 0.5 copy.110
  210.7 0.5 copy-done.3
  211.2 0.3 fusion.3
  211.5 1.2 copy.151
  212.7 1.2 convert_bitcast_fusion
  213.9 0.4 copy.124
  214.3 0.3 fusion.14
  214.6 1.2 copy.150
  215.9 20.0 %all-to-all-done.8 = f32[16,16,8,128]{3,2,1,0:T(8,128)S(1)} async-done(((f32[16,16,8,128]{3,2,1,0:T(8,128)}), f32[16,16,8,128]{3,2,1,0:T(8,128)S(1)}, u32[]{:S(2)}, u32[]{:S(2)}) %all-to-all-start.8) | async-done | bytes 1048608 | tf_op jit(solution)/shard_map/all_to_all | solution.py:16
  235.9 0.6 fusion.21
  (18 shorter events, 0.3 us)
Async XLA Ops:
  0.6 105.9 %copy-start = (bf16[4,128,128]{2,1,0:T(8,128)(2,1)S(1)}, bf16[4,128,128]{2,1,0:T(8,128)(2,1)}, u32[]{:S(2)}) copy-start(bf16[4,128,128]{2,1,0:T(8,128)(2,1)} %param.9) | copy-start | bytes 393220
  0.6 1.4 copy-start.8
  3.6 13.6 %copy-start.2 = (bf16[512,4,128]{2,1,0:T(4,128)(2,1)S(1)}, bf16[512,4,128]{2,1,0:T(4,128)(2,1)}, u32[]{:S(2)}) copy-start(bf16[512,4,128]{2,1,0:T(4,128)(2,1)} %param.11) | copy-start | bytes 1572868
  3.6 31.2 %all-to-all-start = ((bf16[512,4,128]{0,1,2:T(4,128)(2,1)}), bf16[512,4,128]{0,1,2:T(4,128)(2,1)S(1)}, u32[]{:S(2)}, u32[]{:S(2)}) async-start(bf16[512,4,128]{0,1,2:T(4,128)(2,1)} %copy.113), calls=%async_computation | async-start | bytes 1048576 | tf_op jit(solution)/shard_map/all_to_all | solution.py:40
  34.8 22.7 %all-to-all-start.4 = ((bf16[512,4,128]{0,1,2:T(4,128)(2,1)}), bf16[512,4,128]{0,1,2:T(4,128)(2,1)S(1)}, u32[]{:S(2)}, u32[]{:S(2)}) async-start(bf16[512,4,128]{0,1,2:T(4,128)(2,1)} %copy.126), calls=%async_computation.4 | async-start | bytes 1048576 | tf_op jit(solution)/shard_map/all_to_all | solution.py:40
  39.8 0.9 copy-start.6
  57.5 22.7 %all-to-all-start.1 = ((bf16[512,4,128]{0,1,2:T(4,128)(2,1)}), bf16[512,4,128]{0,1,2:T(4,128)(2,1)S(1)}, u32[]{:S(2)}, u32[]{:S(2)}) async-start(bf16[512,4,128]{0,1,2:T(4,128)(2,1)} %copy.116), calls=%async_computation.1 | async-start | bytes 1048576 | tf_op jit(solution)/shard_map/all_to_all | solution.py:40
  62.8 0.9 copy-start.7
  80.2 22.8 %all-to-all-start.5 = ((bf16[512,128,4]{0,2,1:T(4,128)(2,1)}), bf16[512,128,4]{0,2,1:T(4,128)(2,1)}, u32[]{:S(2)}, u32[]{:S(2)}) async-start(bf16[512,128,4]{0,2,1:T(4,128)(2,1)} %copy.129), calls=%async_computation.5 | async-start | bytes 1048576 | tf_op jit(solution)/shard_map/all_to_all | solution.py:44
  106.5 1.3 copy-start.4
  110.1 22.8 %all-to-all-start.6 = ((bf16[512,128,4]{0,2,1:T(4,128)(2,1)}), bf16[512,128,4]{0,2,1:T(4,128)(2,1)}, u32[]{:S(2)}, u32[]{:S(2)}) async-start(bf16[512,128,4]{0,2,1:T(4,128)(2,1)} %copy.135), calls=%async_computation.6 | async-start | bytes 1048576 | tf_op jit(solution)/shard_map/all_to_all | solution.py:44
  132.9 22.7 %all-to-all-start.2 = ((bf16[512,4,128]{0,1,2:T(4,128)(2,1)}), bf16[512,4,128]{0,1,2:T(4,128)(2,1)S(1)}, u32[]{:S(2)}, u32[]{:S(2)}) async-start(bf16[512,4,128]{0,1,2:T(4,128)(2,1)} %copy.120), calls=%async_computation.2 | async-start | bytes 1048576 | tf_op jit(solution)/shard_map/all_to_all | solution.py:40
  155.6 0.8 copy-start.5
  156.3 22.8 %all-to-all-start.7 = ((bf16[512,128,4]{0,2,1:T(4,128)(2,1)}), bf16[512,128,4]{0,2,1:T(4,128)(2,1)}, u32[]{:S(2)}, u32[]{:S(2)}) async-start(bf16[512,128,4]{0,2,1:T(4,128)(2,1)} %copy.138), calls=%async_computation.7 | async-start | bytes 1048576 | tf_op jit(solution)/shard_map/all_to_all | solution.py:44
  179.1 22.8 %all-to-all-start.3 = ((bf16[512,4,128]{0,1,2:T(4,128)(2,1)}), bf16[512,4,128]{0,1,2:T(4,128)(2,1)}, u32[]{:S(2)}, u32[]{:S(2)}) async-start(bf16[512,4,128]{0,1,2:T(4,128)(2,1)} %copy.123), calls=%async_computation.3 | async-start | bytes 1048576 | tf_op jit(solution)/shard_map/all_to_all | solution.py:40
  189.3 20.8 %copy-start.1 = (bf16[512,4,128]{2,1,0:T(4,128)(2,1)S(1)}, bf16[512,4,128]{2,1,0:T(4,128)(2,1)}, u32[]{:S(2)}) copy-start(bf16[512,4,128]{2,1,0:T(4,128)(2,1)} %param.6) | copy-start | bytes 1572868
  201.9 34.0 %all-to-all-start.8 = ((f32[16,16,8,128]{3,2,1,0:T(8,128)}), f32[16,16,8,128]{3,2,1,0:T(8,128)S(1)}, u32[]{:S(2)}, u32[]{:S(2)}) async-start(f32[16,16,8,128]{3,2,1,0:T(8,128)} %copy_bitcast_fusion), calls=%async_computation.8 | async-start | bytes 2097152 | tf_op jit(solution)/shard_map/all_to_all | solution.py:16
  210.1 1.0 copy-start.3
  210.1 1.1 copy-start.9
where the time goes:
time: 238 us; the launch traced here: 237 us
  waiting for transfers between devices  134 us (56%)
  starting transfers between devices  57 us (24%)
  local copies, waits for them, and re-layouts  34.5 us (14%)
  matrix products  7.38 us (3%)
  other arithmetic  3.06 us (1%)
    all_to_all x5, waiting for transfers between devices, forward_swap(): lax.all_to_all(values, 'tensor', split_axis=2, concat_axis=1, tiled=True)  70.1 us
    all_to_all x3, waiting for transfers between devices, backward_swap(): lax.all_to_all(values, 'tensor', split_axis=1, concat_axis=2, tiled=True)  43.6 us
    all_to_all x5, starting transfers between devices, forward_swap(): lax.all_to_all(values, 'tensor', split_axis=2, concat_axis=1, tiled=True)  33.6 us
    all_to_all x1, waiting for transfers between devices, sent_and_summed(): pieces = lax.all_to_all(split_up(x, dim, size), axis, 0, 0, tiled=True)  20 us
    all_to_all x3, starting transfers between devices, backward_swap(): lax.all_to_all(values, 'tensor', split_axis=1, concat_axis=2, tiled=True)  15.2 us
    all_to_all x6, local copies, waits for them, and re-layouts, backward_swap(): lax.all_to_all(values, 'tensor', split_axis=1, concat_axis=2, tiled=True)  8.81 us
    all_to_all x1, starting transfers between devices, sent_and_summed(): pieces = lax.all_to_all(split_up(x, dim, size), axis, 0, 0, tiled=True)  8.2 us
    unnamed x25, local copies, waits for them, and re-layouts  7.94 us
  transfers between devices with their start and end apart: 9, of which 9 were waited for; matrix products, arithmetic and copies ran while one was open for 13% of the time, Pallas kernels for 0%

commit v1 on v0

v1 whole, which is shorter than its diff:
```python
import math

import jax
import jax.numpy as jnp
from jax import lax
from jax.experimental import pallas as pl
from jax.experimental.pallas import tpu as pltpu
from jax.sharding import PartitionSpec as P

BF = jnp.bfloat16
F32 = jnp.float32


def in_to_flat(r):
    return (r & 3) * 128 + (r >> 2)


def flat_to_in(r):
    return (r & 127) * 4 + (r >> 7)


def out_to_flat(r):
    return ((r >> 2) & 3) * 128 + (r >> 4) * 4 + (r & 3)


def flat_to_out(r):
    return ((r & 127) >> 2) * 16 + (r >> 7) * 4 + (r & 3)


def one_hot(col_of_row, cols=512):
    row = lax.broadcasted_iota(jnp.int32, (512, 128), 0)
    col = lax.broadcasted_iota(jnp.int32, (512, 128), 1)
    at = col_of_row(row)
    parts = [jnp.where(at == col + j, 1.0, 0.0).astype(BF) for j in range(0, cols, 128)]
    return jnp.concatenate(parts, axis=1)


def dot(a, b, dims):
    return lax.dot_general(a, b, (dims, ((), ())), preferred_element_type=F32)


def nn(a, b):
    return dot(a, b, ((1,), (0,)))


def nt(a, b):
    return dot(a, b, ((1,), (1,)))


def tn(a, b):
    return dot(a, b, ((0,), (0,)))


def put_rows(ref, first, value):
    ref[:, first : first + 16, :] = value.astype(BF).reshape(32, 16, 512)


def get_rows(ref, first):
    return ref[:, first : first + 16, :].reshape(512, 512)


def by_block(ref):
    return [ref[pl.ds(b, 512, stride=4), :].astype(BF) for b in range(4)]


def right_one_out(r1_ref):
    spread = one_hot(out_to_flat)
    cols = [nt(spread[:, 128 * b : 128 * b + 128], r1_ref[b]).astype(BF) for b in range(4)]
    return jnp.concatenate(cols, axis=1)


def first_kernel(x_ref, g_ref, r1_ref, out_ref, xs_ref, gs_ref):
    xs_ref[...] = x_ref[...].astype(F32)
    gs_ref[...] = g_ref[...].astype(F32)
    x = jnp.concatenate(by_block(xs_ref), axis=1)
    put_rows(out_ref, 0, nt(right_one_out(r1_ref), x))
    g = jnp.concatenate(by_block(gs_ref), axis=1)
    put_rows(out_ref, 16, nt(one_hot(in_to_flat), g))


def weights_kernel(l1_ref, r2_ref, l2_ref, *out_refs):
    spread_in = one_hot(in_to_flat)
    spread_out = one_hot(out_to_flat)
    for n, w_ref in enumerate((l1_ref, r2_ref, l2_ref)):
        parts = [nn(spread_in[:, 128 * b : 128 * b + 128], w_ref[b]).astype(BF) for b in range(4)]
        wide = jnp.concatenate(parts, axis=1)
        out_refs[2 * n][...] = nt(spread_out, wide).astype(BF)
        out_refs[2 * n + 1][...] = nt(wide, spread_out).astype(BF)


def mix_kernel(got_ref, fwd_ref, bwd_ref, out_ref):
    put_rows(out_ref, 0, nn(fwd_ref[...], get_rows(got_ref, 0)))
    put_rows(out_ref, 16, nn(bwd_ref[...], get_rows(got_ref, 16)))


def gelu_kernel(got_ref, fwd_ref, bwd_ref, out_ref, h_ref):
    z = get_rows(got_ref, 0).astype(F32)
    cdf = 0.5 * (1.0 + lax.erf(z * (1.0 / math.sqrt(2.0))))
    h = (z * cdf).astype(BF)
    h_ref[...] = h
    put_rows(out_ref, 0, nn(fwd_ref[...], h))
    slope = cdf + z * jnp.exp(-0.5 * z * z) * (1.0 / math.sqrt(2.0 * math.pi))
    put_rows(out_ref, 16, nn(bwd_ref[...], get_rows(got_ref, 16)) * slope)


def grad_of(fwd, bwd, out_ref):
    a = nn(one_hot(flat_to_in), fwd).astype(BF)
    b = nn(one_hot(flat_to_out), bwd).astype(BF)
    for m in range(4):
        at = slice(128 * m, 128 * m + 128)
        out_ref[m] = nt(a[at], b[at]).astype(BF)


def hidden_grad_kernel(h_ref, got_ref, out_ref):
    grad_of(h_ref[...], get_rows(got_ref, 16), out_ref)


def left_grads_kernel(one_ref, three_ref, l1_ref, l2_ref):
    grad_of(get_rows(one_ref, 0), get_rows(three_ref, 16), l1_ref)
    grad_of(get_rows(three_ref, 0), get_rows(one_ref, 16), l2_ref)


def right_grad_kernel(got_ref, x_ref, l1_ref, r2_ref, l2_ref, out_ref, xs_ref):
    xs_ref[...] = x_ref[...].astype(F32)
    d = nn(one_hot(flat_to_out), get_rows(got_ref, 16)).astype(BF)
    for b, x in enumerate(by_block(xs_ref)):
        g = jnp.transpose(nn(d[128 * b : 128 * b + 128], x))
        out_ref[:, b, :, :] = g.reshape(16, 8, 128).astype(BF)
    for n, ref in enumerate((l1_ref, r2_ref, l2_ref)):
        for b in range(4):
            g = ref[b].astype(F32).reshape(16, 8, 128)
            out_ref[:, 4 * n + 4 + b, :, :] = g.astype(BF)


def last_kernel(got_ref, x_ref, g_ref, r1_ref, out_ref, in_ref, s_ref):
    mixed = tn(get_rows(got_ref, 0), one_hot(in_to_flat))
    for b in range(4):
        s_ref[pl.ds(b, 512, stride=4), :] = mixed[:, 128 * b : 128 * b + 128]
    out_ref[...] = (x_ref[...].astype(F32) + s_ref[...]).astype(BF)
    back = tn(get_rows(got_ref, 16), right_one_out(r1_ref))
    for b in range(4):
        s_ref[pl.ds(b, 512, stride=4), :] = back[:, 128 * b : 128 * b + 128]
    in_ref[...] = (g_ref[...].astype(F32) + s_ref[...]).astype(BF)


def sum_kernel(got_ref, r1_ref, l1_ref, r2_ref, l2_ref):
    for n, ref in enumerate((r1_ref, l1_ref, r2_ref, l2_ref)):
        total = got_ref[0, 4 * n : 4 * n + 4].astype(F32)
        for k in range(1, 16):
            total = total + got_ref[k, 4 * n : 4 * n + 4].astype(F32)
        ref[...] = total


def call(kernel, shapes, *args, scratch=()):
    outs = [jax.ShapeDtypeStruct(s, d) for s, d in shapes]
    with jax.named_scope(kernel.__name__):
        return pl.pallas_call(
            kernel,
            out_shape=outs,
            scratch_shapes=[pltpu.VMEM(s, F32) for s in scratch],
            name=kernel.__name__,
        )(*args)


def swap(x, axis):
    return lax.all_to_all(x, axis, 0, 0, tiled=True)


def on_device(tokens_in, right_one, left_one, right_two, left_two, out_grad):
    x = tokens_in.reshape(2048, 128)
    g = out_grad.reshape(2048, 128)
    chunk = ((32, 32, 512), BF)
    square = ((512, 512), BF)
    grad = ((4, 128, 128), BF)
    rows = (2048, 128)
    (send,) = call(first_kernel, [chunk], x, g, right_one, scratch=(rows, rows))
    one = swap(send, "tensor")
    l1t, l1n, r2t, r2n, l2t, l2n = call(weights_kernel, [square] * 6, left_one, right_two, left_two)
    (send,) = call(mix_kernel, [chunk], one, l1t, l2n)
    two = swap(send, "tensor")
    send, h = call(gelu_kernel, [chunk, square], two, r2t, r2n)
    three = swap(send, "tensor")
    (gr2,) = call(hidden_grad_kernel, [grad], h, two)
    (send,) = call(mix_kernel, [chunk], three, l2t, l1n)
    four = swap(send, "tensor")
    gl1, gl2 = call(left_grads_kernel, [grad] * 2, one, three)
    (send,) = call(right_grad_kernel, [((16, 16, 8, 128), BF)], four, x, gl1, gr2, gl2, scratch=(rows,))
    sums = swap(send, "dp")
    layer_out, input_grad = call(last_kernel, [(rows, BF)] * 2, four, x, g, right_one, scratch=(rows,))
    grads = call(sum_kernel, [((4, 8, 128), F32)] * 4, sums)
    return (layer_out.reshape(512, 4, 128), input_grad.reshape(512, 4, 128), *grads)


def solution(mesh):
    placed = (
        P("dp", "tensor", None),
        P("tensor", None, None),
        P("tensor", None, None),
        P("tensor", None, None),
        P("tensor", None, None),
        P("dp", "tensor", None),
    )
    return jax.shard_map(
        on_device,
        mesh=mesh,
        in_specs=placed,
        out_specs=(
            P("dp", "tensor", None),
            P("dp", "tensor", None),
            P("tensor", "dp", None),
            P("tensor", "dp", None),
            P("tensor", "dp", None),
            P("tensor", "dp", None),
        ),
        check_vma=False,
    )
```

time: 238 us -> 190 us (0.80)
  the two profiles are of different devices: /device:TPU:12 before, /device:TPU:14 now
where the time goes in v1:
time: 190 us; the launch traced here: 189 us
  blocking collectives  68 us (36%)
  waiting for transfers between devices  58.3 us (31%)
  Pallas kernels  32.1 us (17%)
  starting transfers between devices  26.9 us (14%)
  local copies, waits for them, and re-layouts  2.74 us (1%)
    all_to_all x2, blocking collectives, swap(): return lax.all_to_all(x, axis, 0, 0, tiled=True)  68 us
    all_to_all x3, waiting for transfers between devices, swap(): return lax.all_to_all(x, axis, 0, 0, tiled=True)  58.3 us
    pallas_call x10, Pallas kernels, call(): pl.pallas_call(kernel, out_shape=outs, scratch_shapes=[pltpu.VMEM(s, F32)...  32.1 us
    all_to_all x3, starting transfers between devices, swap(): return lax.all_to_all(x, axis, 0, 0, tiled=True)  26.9 us
  transfers between devices with their start and end apart: 3, of which 3 were waited for; matrix products, arithmetic and copies ran while one was open for 0% of the time, Pallas kernels for 8%

profile of v1, /device:TPU:14, one launch (start us, length us, event | category | flops | bytes accessed | tf_op | source)
XLA Modules:
  0.0 188.7 jit_solution(6363047300794415210)
XLA Ops:
  0.6 3.1 %first_kernel.1 = bf16[32,32,512]{2,1,0:T(8,128)(2,1)} custom-call(bf16[2048,128]{1,0:T(8,128)(2,1)} %bitcast.4, bf16[2048,128]{1,0:T(8,128)(2,1)} %bitcast.7, bf16[4,128,128]{2,1,0:T(8,128)(2,1)} %r1_ref.3), custom_call_target="tpu_custom_call" | custom-call | tf_op jit(solution)/shard_map/first_kernel/first_kernel/pallas_call | solution.py:157
  3.8 13.4 %all-to-all-start = ((bf16[32,32,512]{2,1,0:T(8,128)(2,1)}), bf16[32,32,512]{2,1,0:T(8,128)(2,1)S(1)}, u32[]{:S(2)}, u32[]{:S(2)}) async-start(bf16[32,32,512]{2,1,0:T(8,128)(2,1)} %first_kernel.1), calls=%async_computation | async-start | bytes 2097152 | tf_op jit(solution)/shard_map/all_to_all | solution.py:166
  17.2 4.3 %weights_kernel.1 = (bf16[512,512]{1,0:T(8,128)(2,1)}, bf16[512,512]{1,0:T(8,128)(2,1)}, bf16[512,512]{1,0:T(8,128)(2,1)}, bf16[512,512]{1,0:T(8,128)(2,1)}, bf1...) custom-call(bf16[4,128,128]{2,1,0:T(8,128)(2,1)} %l1_ref.1, bf16[4,128,128]{2,1,0:T(8,128)(2,1)} %r2_ref.1, ...), custom_call_target="tpu_custom_call" | custom-call | tf_op jit(solution)/shard_map/weights_kernel/weights_kernel/pallas_call | solution.py:157
  21.5 24.6 %all-to-all-done.got_ref.one_ref = bf16[32,32,512]{2,1,0:T(8,128)(2,1)S(1)} async-done(((bf16[32,32,512]{2,1,0:T(8,128)(2,1)}), bf16[32,32,512]{2,1,0:T(8,128)(2,1)S(1)}, u32[]{:S(2)}, u32[]{:S(2)}) %all-to-all-start) | async-done | bytes 1048608 | tf_op jit(solution)/shard_map/all_to_all | solution.py:166
  46.1 0.0 copy-start
  46.1 1.0 copy-done
  47.1 3.2 %mix_kernel.2 = bf16[32,32,512]{2,1,0:T(8,128)(2,1)} custom-call(bf16[32,32,512]{2,1,0:T(8,128)(2,1)} %copy-done, bf16[512,512]{1,0:T(8,128)(2,1)} %get-tuple-element.22.fwd_ref, bf16[512,512]{1,0:T(8,128)(2,1)} %get-tuple-element.23.bwd_ref), custom_call_target="tpu_custom_call" | custom-call | tf_op jit(solution)/shard_map/mix_kernel/mix_kernel/pallas_call | solution.py:157
  50.3 34.0 %all_to_all.25.got_ref = bf16[32,32,512]{2,1,0:T(8,128)(2,1)} all-to-all(bf16[32,32,512]{2,1,0:T(8,128)(2,1)} %mix_kernel.2), channel_id=1, replica_groups=mesh['dp'=16,'tensor'=32] {'tensor'}, dimensions={0} | all-to-all | bytes 2097152 | tf_op jit(solution)/shard_map/all_to_all | solution.py:166
  84.3 3.4 %gelu_kernel.1 = (bf16[32,32,512]{2,1,0:T(8,128)(2,1)}, bf16[512,512]{1,0:T(8,128)(2,1)}) custom-call(bf16[32,32,512]{2,1,0:T(8,128)(2,1)} %all_to_all.25.got_ref, bf16[512,512]{1,0:T(8,128)(2,1)} %get-tuple-element.24.fwd_ref, bf16[512,512]{1,0:T(8,128)(2,1)} %get-tuple-element.25.bwd_ref), custom_call_target="tpu_custom_call" | custom-call | tf_op jit(solution)/shard_map/gelu_kernel/gelu_kernel/pallas_call | solution.py:157
  87.7 34.0 %all_to_all.26.got_ref.three_ref = bf16[32,32,512]{2,1,0:T(8,128)(2,1)} all-to-all(bf16[32,32,512]{2,1,0:T(8,128)(2,1)} %get-tuple-element.26), channel_id=1, replica_groups=mesh['dp'=16,'tensor'=32] {'tensor'}, dimensions={0} | all-to-all | bytes 2097152 | tf_op jit(solution)/shard_map/all_to_all | solution.py:166
  121.7 3.2 %mix_kernel.3 = bf16[32,32,512]{2,1,0:T(8,128)(2,1)} custom-call(bf16[32,32,512]{2,1,0:T(8,128)(2,1)} %all_to_all.26.got_ref.three_ref, bf16[512,512]{1,0:T(8,128)(2,1)} %get-tuple-element.27.fwd_ref, bf16[512,512]{1,0:T(8,128)(2,1)} %get-tuple-element.28.bwd_ref), custom_call_target="tpu_custom_call" | custom-call | tf_op jit(solution)/shard_map/mix_kernel/mix_kernel/pallas_call | solution.py:157
  124.9 5.0 %all-to-all-start.3 = ((bf16[32,32,512]{2,1,0:T(8,128)(2,1)}), bf16[32,32,512]{2,1,0:T(8,128)(2,1)S(1)}, u32[]{:S(2)}, u32[]{:S(2)}) async-start(bf16[32,32,512]{2,1,0:T(8,128)(2,1)} %mix_kernel.3), calls=%async_computation.3 | async-start | bytes 2097152 | tf_op jit(solution)/shard_map/all_to_all | solution.py:166
  129.9 2.9 %hidden_grad_kernel.1.r2_ref = bf16[4,128,128]{2,1,0:T(8,128)(2,1)} custom-call(bf16[512,512]{1,0:T(8,128)(2,1)} %get-tuple-element.32.h_ref, bf16[32,32,512]{2,1,0:T(8,128)(2,1)} %all_to_all.25.got_ref), custom_call_target="tpu_custom_call" | custom-call | tf_op jit(solution)/shard_map/hidden_grad_kernel/hidden_grad_kernel/pallas_call | solution.py:157
  132.8 3.8 %left_grads_kernel.1 = (bf16[4,128,128]{2,1,0:T(8,128)(2,1)}, bf16[4,128,128]{2,1,0:T(8,128)(2,1)}) custom-call(bf16[32,32,512]{2,1,0:T(8,128)(2,1)} %copy-done, bf16[32,32,512]{2,1,0:T(8,128)(2,1)} %all_to_all.26.got_ref.three_ref), custom_call_target="tpu_custom_call" | custom-call | tf_op jit(solution)/shard_map/left_grads_kernel/left_grads_kernel/pallas_call | solution.py:157
  136.6 22.2 %all-to-all-done.3.got_ref = bf16[32,32,512]{2,1,0:T(8,128)(2,1)S(1)} async-done(((bf16[32,32,512]{2,1,0:T(8,128)(2,1)}), bf16[32,32,512]{2,1,0:T(8,128)(2,1)S(1)}, u32[]{:S(2)}, u32[]{:S(2)}) %all-to-all-start.3) | async-done | bytes 1048608 | tf_op jit(solution)/shard_map/all_to_all | solution.py:166
  158.8 0.0 copy-start.1
  158.8 1.0 copy-done.1
  159.8 3.0 %right_grad_kernel.1 = bf16[16,16,8,128]{3,2,1,0:T(8,128)(2,1)} custom-call(bf16[32,32,512]{2,1,0:T(8,128)(2,1)} %copy-done.1, bf16[2048,128]{1,0:T(8,128)(2,1)} %bitcast.5, bf16[4,128,128]{2,1,0:T(8,128)(2,1)} %get-tuple-element.31.l1_ref, bf16[4,128,128]{2,1,0:T(8,128)(2,1)} %hidden_grad_kernel.1.r2_ref, bf16[4,128,128]{2,1,0:T(8,128)(2,1)} %get-tuple-element.33.l2_ref), custom_call_target="tpu_custom_call" | custom-call | tf_op jit(solution)/shard_map/right_grad_kernel/right_grad_kernel/pallas_call | solution.py:157
  162.7 8.5 %all-to-all-start.4 = ((bf16[16,16,8,128]{3,2,1,0:T(8,128)(2,1)}), bf16[16,16,8,128]{3,2,1,0:T(8,128)(2,1)S(1)}, u32[]{:S(2)}, u32[]{:S(2)}) async-start(bf16[16,16,8,128]{3,2,1,0:T(8,128)(2,1)} %right_grad_kernel.1), calls=%async_computation.4 | async-start | bytes 1048576 | tf_op jit(solution)/shard_map/all_to_all | solution.py:166
  171.2 3.4 %last_kernel.1 = (bf16[2048,128]{1,0:T(8,128)(2,1)}, bf16[2048,128]{1,0:T(8,128)(2,1)}) custom-call(bf16[32,32,512]{2,1,0:T(8,128)(2,1)} %copy-done.1, bf16[2048,128]{1,0:T(8,128)(2,1)} %bitcast.6, bf16[2048,128]{1,0:T(8,128)(2,1)} %bitcast.8, bf16[4,128,128]{2,1,0:T(8,128)(2,1)} %r1_ref.3), custom_call_target="tpu_custom_call" | custom-call | tf_op jit(solution)/shard_map/last_kernel/last_kernel/pallas_call | solution.py:157
  174.6 11.6 %all-to-all-done.4.got_ref = bf16[16,16,8,128]{3,2,1,0:T(8,128)(2,1)S(1)} async-done(((bf16[16,16,8,128]{3,2,1,0:T(8,128)(2,1)}), bf16[16,16,8,128]{3,2,1,0:T(8,128)(2,1)S(1)}, u32[]{:S(2)}, u32[]{:S(2)}) %all-to-all-start.4) | async-done | bytes 524320 | tf_op jit(solution)/shard_map/all_to_all | solution.py:166
  186.2 0.0 copy-start.2
  186.2 0.8 copy-done.2
  187.0 1.7 sum_kernel.1
Async XLA Ops:
  3.8 42.4 %all-to-all-start = ((bf16[32,32,512]{2,1,0:T(8,128)(2,1)}), bf16[32,32,512]{2,1,0:T(8,128)(2,1)S(1)}, u32[]{:S(2)}, u32[]{:S(2)}) async-start(bf16[32,32,512]{2,1,0:T(8,128)(2,1)} %first_kernel.1), calls=%async_computation | async-start | bytes 2097152 | tf_op jit(solution)/shard_map/all_to_all | solution.py:166
  46.1 1.0 copy-start
  124.9 33.9 %all-to-all-start.3 = ((bf16[32,32,512]{2,1,0:T(8,128)(2,1)}), bf16[32,32,512]{2,1,0:T(8,128)(2,1)S(1)}, u32[]{:S(2)}, u32[]{:S(2)}) async-start(bf16[32,32,512]{2,1,0:T(8,128)(2,1)} %mix_kernel.3), calls=%async_computation.3 | async-start | bytes 2097152 | tf_op jit(solution)/shard_map/all_to_all | solution.py:166
  158.8 1.0 copy-start.1
  162.7 23.5 %all-to-all-start.4 = ((bf16[16,16,8,128]{3,2,1,0:T(8,128)(2,1)}), bf16[16,16,8,128]{3,2,1,0:T(8,128)(2,1)S(1)}, u32[]{:S(2)}, u32[]{:S(2)}) async-start(bf16[16,16,8,128]{3,2,1,0:T(8,128)(2,1)} %right_grad_kernel.1), calls=%async_computation.4 | async-start | bytes 1048576 | tf_op jit(solution)/shard_map/all_to_all | solution.py:166
  186.2 0.8 copy-start.2

commit v2 on v1

--- a/solution.py
+++ b/solution.py
@@ -69,23 +69,36 @@
     return jnp.concatenate(cols, axis=1)
 
 
-def first_kernel(x_ref, g_ref, r1_ref, out_ref, xs_ref, gs_ref):
+def fetch(pairs, sems):
+    copies = [pltpu.make_async_copy(src, dst, sems.at[n]) for n, (src, dst) in enumerate(pairs)]
+    for copy in copies:
+        copy.start()
+    return copies
+
+
+def first_kernel(x_hbm, g_hbm, r1_hbm, out_ref, xs_ref, gs_ref, x_ref, g_ref, r1_ref, sems):
+    r1_in, x_in, g_in = fetch(((r1_hbm, r1_ref), (x_hbm, x_ref), (g_hbm, g_ref)), sems)
+    order = one_hot(in_to_flat)
+    r1_in.wait()
+    wide = right_one_out(r1_ref)
+    x_in.wait()
     xs_ref[...] = x_ref[...].astype(F32)
+    put_rows(out_ref, 0, nt(wide, jnp.concatenate(by_block(xs_ref), axis=1)))
+    g_in.wait()
     gs_ref[...] = g_ref[...].astype(F32)
-    x = jnp.concatenate(by_block(xs_ref), axis=1)
-    put_rows(out_ref, 0, nt(right_one_out(r1_ref), x))
-    g = jnp.concatenate(by_block(gs_ref), axis=1)
-    put_rows(out_ref, 16, nt(one_hot(in_to_flat), g))
-
-
-def weights_kernel(l1_ref, r2_ref, l2_ref, *out_refs):
+    put_rows(out_ref, 16, nt(order, jnp.concatenate(by_block(gs_ref), axis=1)))
+
+
+def widen(w_ref, spread_in):
+    parts = [nn(spread_in[:, 128 * b : 128 * b + 128], w_ref[b]).astype(BF) for b in range(4)]
+    return jnp.concatenate(parts, axis=1)
+
+
+def weights_kernel(fwd_ref, bwd_ref, fwd_out, bwd_out):
     spread_in = one_hot(in_to_flat)
     spread_out = one_hot(out_to_flat)
-    for n, w_ref in enumerate((l1_ref, r2_ref, l2_ref)):
-        parts = [nn(spread_in[:, 128 * b : 128 * b + 128], w_ref[b]).astype(BF) for b in range(4)]
-        wide = jnp.concatenate(parts, axis=1)
-        out_refs[2 * n][...] = nt(spread_out, wide).astype(BF)
-        out_refs[2 * n + 1][...] = nt(wide, spread_out).astype(BF)
+    fwd_out[...] = nt(spread_out, widen(fwd_ref, spread_in)).astype(BF)
+    bwd_out[...] = nt(widen(bwd_ref, spread_in), spread_out).astype(BF)
 
 
 def mix_kernel(got_ref, fwd_ref, bwd_ref, out_ref):
@@ -111,25 +124,31 @@
         out_ref[m] = nt(a[at], b[at]).astype(BF)
 
 
-def hidden_grad_kernel(h_ref, got_ref, out_ref):
+def hidden_grad_kernel(h_ref, got_hbm, out_ref, got_ref, sems):
+    (got_in,) = fetch(((got_hbm, got_ref),), sems)
+    got_in.wait()
     grad_of(h_ref[...], get_rows(got_ref, 16), out_ref)
 
 
-def left_grads_kernel(one_ref, three_ref, l1_ref, l2_ref):
+def left_grads_kernel(one_hbm, three_hbm, l1_ref, l2_ref, one_ref, three_ref, sems):
+    for copy in fetch(((one_hbm, one_ref), (three_hbm, three_ref)), sems):
+        copy.wait()
     grad_of(get_rows(one_ref, 0), get_rows(three_ref, 16), l1_ref)
     grad_of(get_rows(three_ref, 0), get_rows(one_ref, 16), l2_ref)
 
 
-def right_grad_kernel(got_ref, x_ref, l1_ref, r2_ref, l2_ref, out_ref, xs_ref):
-    xs_ref[...] = x_ref[...].astype(F32)
-    d = nn(one_hot(flat_to_out), get_rows(got_ref, 16)).astype(BF)
-    for b, x in enumerate(by_block(xs_ref)):
-        g = jnp.transpose(nn(d[128 * b : 128 * b + 128], x))
-        out_ref[:, b, :, :] = g.reshape(16, 8, 128).astype(BF)
+def right_grad_kernel(got_ref, x_hbm, l1_ref, r2_ref, l2_ref, out_ref, xs_ref, x_ref, sems):
+    (x_in,) = fetch(((x_hbm, x_ref),), sems)
     for n, ref in enumerate((l1_ref, r2_ref, l2_ref)):
         for b in range(4):
             g = ref[b].astype(F32).reshape(16, 8, 128)
             out_ref[:, 4 * n + 4 + b, :, :] = g.astype(BF)
+    d = nn(one_hot(flat_to_out), get_rows(got_ref, 16)).astype(BF)
+    x_in.wait()
+    xs_ref[...] = x_ref[...].astype(F32)
+    for b, x in enumerate(by_block(xs_ref)):
+        g = jnp.transpose(nn(d[128 * b : 128 * b + 128], x))
+        out_ref[:, b, :, :] = g.reshape(16, 8, 128).astype(BF)
 
 
 def last_kernel(got_ref, x_ref, g_ref, r1_ref, out_ref, in_ref, s_ref):
@@ -151,14 +170,24 @@
         ref[...] = total
 
 
-def call(kernel, shapes, *args, scratch=()):
+ROWS = (2048, 128)
+WIDE_ROWS = pltpu.VMEM(ROWS, F32)
+HALF_ROWS = pltpu.VMEM(ROWS, BF)
+CHUNK = pltpu.VMEM((32, 32, 512), BF)
+
+
+def call(kernel, shapes, *args, scratch=(), far=()):
+    args = [pltpu.with_memory_space_constraint(a, pltpu.HBM) if n in far else a for n, a in enumerate(args)]
     outs = [jax.ShapeDtypeStruct(s, d) for s, d in shapes]
+    specs = [pl.BlockSpec(memory_space=pltpu.HBM if n in far else pltpu.VMEM) for n in range(len(args))]
     with jax.named_scope(kernel.__name__):
         return pl.pallas_call(
             kernel,
             out_shape=outs,
-            scratch_shapes=[pltpu.VMEM(s, F32) for s in scratch],
+            in_specs=specs,
+            scratch_shapes=scratch,
             name=kernel.__name__,
+            compiler_params=pltpu.CompilerParams(vmem_limit_bytes=16 << 20),
         )(*args)
 
 
@@ -166,27 +195,77 @@
     return lax.all_to_all(x, axis, 0, 0, tiled=True)
 
 
+def after(first, *values):
+    return lax.optimization_barrier((first, *values))[1:]
+
+
 def on_device(tokens_in, right_one, left_one, right_two, left_two, out_grad):
-    x = tokens_in.reshape(2048, 128)
-    g = out_grad.reshape(2048, 128)
+    x = tokens_in.reshape(ROWS)
+    g = out_grad.reshape(ROWS)
     chunk = ((32, 32, 512), BF)
     square = ((512, 512), BF)
     grad = ((4, 128, 128), BF)
-    rows = (2048, 128)
-    (send,) = call(first_kernel, [chunk], x, g, right_one, scratch=(rows, rows))
+    (send,) = call(
+        first_kernel,
+        [chunk],
+        x,
+        g,
+        right_one,
+        scratch=(
+            WIDE_ROWS,
+            WIDE_ROWS,
+            HALF_ROWS,
+            HALF_ROWS,
+            pltpu.VMEM((4, 128, 128), BF),
+            pltpu.SemaphoreType.DMA((3,)),
+        ),
+        far=(0, 1, 2),
+    )
     one = swap(send, "tensor")
-    l1t, l1n, r2t, r2n, l2t, l2n = call(weights_kernel, [square] * 6, left_one, right_two, left_two)
-    (send,) = call(mix_kernel, [chunk], one, l1t, l2n)
+    fwd, bwd = call(weights_kernel, [square] * 2, *after(send, left_one, left_two))
+    (send,) = call(mix_kernel, [chunk], one, fwd, bwd)
+    (one,) = after(send, one)
     two = swap(send, "tensor")
-    send, h = call(gelu_kernel, [chunk, square], two, r2t, r2n)
+    fwd, bwd = call(weights_kernel, [square] * 2, *after(send, right_two, right_two))
+    send, h = call(gelu_kernel, [chunk, square], two, fwd, bwd)
+    h, two = after(send, h, two)
     three = swap(send, "tensor")
-    (gr2,) = call(hidden_grad_kernel, [grad], h, two)
-    (send,) = call(mix_kernel, [chunk], three, l2t, l1n)
+    fwd, bwd = call(weights_kernel, [square] * 2, *after(send, left_two, left_one))
+    (gr2,) = call(
+        hidden_grad_kernel,
+        [grad],
+        h,
+        two,
+        scratch=(CHUNK, pltpu.SemaphoreType.DMA((1,))),
+        far=(1,),
+    )
+    three, gr2 = lax.optimization_barrier((three, gr2))
+    (send,) = call(mix_kernel, [chunk], three, fwd, bwd)
+    (three,) = after(send, three)
     four = swap(send, "tensor")
-    gl1, gl2 = call(left_grads_kernel, [grad] * 2, one, three)
-    (send,) = call(right_grad_kernel, [((16, 16, 8, 128), BF)], four, x, gl1, gr2, gl2, scratch=(rows,))
+    gl1, gl2 = call(
+        left_grads_kernel,
+        [grad] * 2,
+        one,
+        three,
+        scratch=(CHUNK, CHUNK, pltpu.SemaphoreType.DMA((2,))),
+        far=(0, 1),
+    )
+    (send,) = call(
+        right_grad_kernel,
+        [((16, 16, 8, 128), BF)],
+        four,
+        x,
+        gl1,
+        gr2,
+        gl2,
+        scratch=(WIDE_ROWS, HALF_ROWS, pltpu.SemaphoreType.DMA((1,))),
+        far=(1,),
+    )
     sums = swap(send, "dp")
-    layer_out, input_grad = call(last_kernel, [(rows, BF)] * 2, four, x, g, right_one, scratch=(rows,))
+    layer_out, input_grad = call(
+        last_kernel, [(ROWS, BF)] * 2, four, x, g, right_one, scratch=(WIDE_ROWS,)
+    )
     grads = call(sum_kernel, [((4, 8, 128), F32)] * 4, sums)
     return (layer_out.reshape(512, 4, 128), input_grad.reshape(512, 4, 128), *grads)
 

time: 190 us -> 181 us (0.953)
  blocking collectives: 68 us -> 0 us
  waiting for transfers between devices: 58.3 us -> 120 us
  starting transfers between devices: 26.9 us -> 37.3 us
  Pallas kernels: 32.1 us -> 22.2 us
  local copies, waits for them, and re-layouts: 2.74 us -> 0.04 us
    all_to_all x2 -> x0, blocking collectives: 68 us -> none  [swap(): return lax.all_to_all(x, axis, 0, 0, tiled=True)]
    all_to_all x3 -> x5, waiting for transfers between devices: 58.3 us -> 120 us  [swap(): return lax.all_to_all(x, axis, 0, 0, tiled=True)]
    all_to_all x3 -> x5, starting transfers between devices: 26.9 us -> 37.3 us  [swap(): return lax.all_to_all(x, axis, 0, 0, tiled=True)]
    pallas_call x10 -> x12, Pallas kernels: 32.1 us -> 22.2 us  [call(): pl.pallas_call(kernel, out_shape=outs, in_specs=specs, scratch_shapes=scr...]
    unnamed x6 -> x18, local copies, waits for them, and re-layouts: 2.74 us -> 0.04 us
  transfers between devices with their start and end apart: 3 -> 5, of which waited for: 3 -> 5; matrix products, arithmetic and copies ran while one was open for 0% -> 0% of each run, Pallas kernels for 8% -> 6%
where the time goes in v2:
time: 181 us; the launch traced here: 180 us
  waiting for transfers between devices  120 us (66%)
  starting transfers between devices  37.3 us (21%)
  Pallas kernels  22.2 us (12%)
    all_to_all x5, waiting for transfers between devices, swap(): return lax.all_to_all(x, axis, 0, 0, tiled=True)  120 us
    all_to_all x5, starting transfers between devices, swap(): return lax.all_to_all(x, axis, 0, 0, tiled=True)  37.3 us
    pallas_call x12, Pallas kernels, call(): pl.pallas_call(kernel, out_shape=outs, in_specs=specs, scratch_shapes=scr...  22.2 us
  transfers between devices with their start and end apart: 5, of which 5 were waited for; matrix products, arithmetic and copies ran while one was open for 0% of the time, Pallas kernels for 6%

profile of v2, /device:TPU:14, one launch (start us, length us, event | category | flops | bytes accessed | tf_op | source)
XLA Modules:
  0.0 180.4 jit_solution(13157422890792675040)
XLA Ops:
  0.6 3.3 %first_kernel.1 = bf16[32,32,512]{2,1,0:T(8,128)(2,1)} custom-call(bf16[2048,128]{1,0:T(8,128)(2,1)} %bitcast.4, bf16[2048,128]{1,0:T(8,128)(2,1)} %bitcast.7, bf16[4,128,128]{2,1,0:T(8,128)(2,1)} %r1_ref.1), custom_call_target="tpu_custom_call" | custom-call | tf_op jit(solution)/shard_map/first_kernel/first_kernel/pallas_call | solution.py:184
  3.9 0.0 copy-start.7
  3.9 0.0 copy-start.8
  4.0 13.6 %all-to-all-start = ((bf16[32,32,512]{2,1,0:T(8,128)(2,1)}), bf16[32,32,512]{2,1,0:T(8,128)(2,1)S(1)}, u32[]{:S(2)}, u32[]{:S(2)}) async-start(bf16[32,32,512]{2,1,0:T(8,128)(2,1)} %first_kernel.1), calls=%async_computation | async-start | bytes 2097152 | tf_op jit(solution)/shard_map/all_to_all | solution.py:195
  17.5 0.0 copy-done.7
  17.6 0.0 copy-done.8
  17.6 1.1 weights_kernel.3
  18.7 27.8 %all-to-all-done.got_ref.one_hbm = bf16[32,32,512]{2,1,0:T(8,128)(2,1)S(1)} async-done(((bf16[32,32,512]{2,1,0:T(8,128)(2,1)}), bf16[32,32,512]{2,1,0:T(8,128)(2,1)S(1)}, u32[]{:S(2)}, u32[]{:S(2)}) %all-to-all-start) | async-done | bytes 1048608 | tf_op jit(solution)/shard_map/all_to_all | solution.py:195
  46.5 0.0 copy-start
  46.5 1.7 mix_kernel.2
  48.1 0.0 copy-done
  48.1 0.0 copy-start.6
  48.1 5.1 %all-to-all-start.1 = ((bf16[32,32,512]{2,1,0:T(8,128)(2,1)}), bf16[32,32,512]{2,1,0:T(8,128)(2,1)S(1)}, u32[]{:S(2)}, u32[]{:S(2)}) async-start(bf16[32,32,512]{2,1,0:T(8,128)(2,1)} %mix_kernel.2), calls=%async_computation.1 | async-start | bytes 2097152 | tf_op jit(solution)/shard_map/all_to_all | solution.py:195
  53.3 0.0 copy-done.6
  53.3 1.1 weights_kernel.4
  54.4 27.8 %all-to-all-done.1.got_ref.got_hbm = bf16[32,32,512]{2,1,0:T(8,128)(2,1)S(1)} async-done(((bf16[32,32,512]{2,1,0:T(8,128)(2,1)}), bf16[32,32,512]{2,1,0:T(8,128)(2,1)S(1)}, u32[]{:S(2)}, u32[]{:S(2)}) %all-to-all-start.1) | async-done | bytes 1048608 | tf_op jit(solution)/shard_map/all_to_all | solution.py:195
  82.2 0.0 copy-start.2
  82.2 1.9 %gelu_kernel.1 = (bf16[32,32,512]{2,1,0:T(8,128)(2,1)}, bf16[512,512]{1,0:T(8,128)(2,1)S(1)}) custom-call(bf16[32,32,512]{2,1,0:T(8,128)(2,1)S(1)} %all-to-all-done.1.got_ref.got_hbm, bf16[512,512]{1,0:T(8,128)(2,1)S(1)} %get-tuple-element.40.fwd_ref, bf16[512,512]{1,0:T(8,128)(2,1)S(1)} %get-tuple-element.41.bwd_ref), custom_call_target="tpu_custom_call" | custom-call | tf_op jit(solution)/shard_map/gelu_kernel/gelu_kernel/pallas_call | solution.py:184
  84.0 0.0 copy-done.2
  84.1 5.0 %all-to-all-start.2 = ((bf16[32,32,512]{2,1,0:T(8,128)(2,1)}), bf16[32,32,512]{2,1,0:T(8,128)(2,1)S(1)}, u32[]{:S(2)}, u32[]{:S(2)}) async-start(bf16[32,32,512]{2,1,0:T(8,128)(2,1)} %get-tuple-element.42), calls=%async_computation.2 | async-start | bytes 2097152 | tf_op jit(solution)/shard_map/all_to_all | solution.py:195
  89.0 2.2 %hidden_grad_kernel.1.r2_ref = bf16[4,128,128]{2,1,0:T(8,128)(2,1)S(1)} custom-call(bf16[512,512]{1,0:T(8,128)(2,1)S(1)} %get-tuple-element.44.h_ref, bf16[32,32,512]{2,1,0:T(8,128)(2,1)} %copy-done.2), custom_call_target="tpu_custom_call" | custom-call | tf_op jit(solution)/shard_map/hidden_grad_kernel/hidden_grad_kernel/pallas_call | solution.py:184
  91.2 1.1 weights_kernel.5
  92.3 25.7 %all-to-all-done.2.got_ref.three_hbm = bf16[32,32,512]{2,1,0:T(8,128)(2,1)S(1)} async-done(((bf16[32,32,512]{2,1,0:T(8,128)(2,1)}), bf16[32,32,512]{2,1,0:T(8,128)(2,1)S(1)}, u32[]{:S(2)}, u32[]{:S(2)}) %all-to-all-start.2) | async-done | bytes 1048608 | tf_op jit(solution)/shard_map/all_to_all | solution.py:195
  118.0 0.0 copy-start.1
  118.0 1.7 mix_kernel.3
  119.6 0.0 copy-done.1
  119.6 5.0 %all-to-all-start.3 = ((bf16[32,32,512]{2,1,0:T(8,128)(2,1)}), bf16[32,32,512]{2,1,0:T(8,128)(2,1)S(1)}, u32[]{:S(2)}, u32[]{:S(2)}) async-start(bf16[32,32,512]{2,1,0:T(8,128)(2,1)} %mix_kernel.3), calls=%async_computation.3 | async-start | bytes 2097152 | tf_op jit(solution)/shard_map/all_to_all | solution.py:195
  124.6 3.2 %left_grads_kernel.1 = (bf16[4,128,128]{2,1,0:T(8,128)(2,1)S(1)}, bf16[4,128,128]{2,1,0:T(8,128)(2,1)S(1)}) custom-call(bf16[32,32,512]{2,1,0:T(8,128)(2,1)} %copy-done, bf16[32,32,512]{2,1,0:T(8,128)(2,1)} %copy-done.1), custom_call_target="tpu_custom_call" | custom-call | tf_op jit(solution)/shard_map/left_grads_kernel/left_grads_kernel/pallas_call | solution.py:184
  127.8 25.7 %all-to-all-done.3.got_ref = bf16[32,32,512]{2,1,0:T(8,128)(2,1)S(1)} async-done(((bf16[32,32,512]{2,1,0:T(8,128)(2,1)}), bf16[32,32,512]{2,1,0:T(8,128)(2,1)S(1)}, u32[]{:S(2)}, u32[]{:S(2)}) %all-to-all-start.3) | async-done | bytes 1048608 | tf_op jit(solution)/shard_map/all_to_all | solution.py:195
  153.5 0.0 copy-start.5
  153.5 2.5 %right_grad_kernel.1 = bf16[16,16,8,128]{3,2,1,0:T(8,128)(2,1)} custom-call(bf16[32,32,512]{2,1,0:T(8,128)(2,1)S(1)} %all-to-all-done.3.got_ref, bf16[2048,128]{1,0:T(8,128)(2,1)} %bitcast.5, bf16[4,128,128]{2,1,0:T(8,128)(2,1)S(1)} %get-tuple-element.55.l1_ref, bf16[4,128,128]{2,1,0:T(8,128)(2,1)S(1)} %hidden_grad_kernel.1.r2_ref, ...), custom_call_target="tpu_custom_call" | custom-call | tf_op jit(solution)/shard_map/right_grad_kernel/right_grad_kernel/pallas_call | solution.py:184
  156.1 0.0 copy-start.3
  156.1 0.0 copy-start.4
  156.1 8.6 %all-to-all-start.4 = ((bf16[16,16,8,128]{3,2,1,0:T(8,128)(2,1)}), bf16[16,16,8,128]{3,2,1,0:T(8,128)(2,1)S(1)}, u32[]{:S(2)}, u32[]{:S(2)}) async-start(bf16[16,16,8,128]{3,2,1,0:T(8,128)(2,1)} %right_grad_kernel.1), calls=%async_computation.4 | async-start | bytes 1048576 | tf_op jit(solution)/shard_map/all_to_all | solution.py:195
  164.7 0.0 copy-done.5
  164.7 0.0 copy-done.3
  164.7 0.0 copy-done.4
  164.7 1.9 %last_kernel.1 = (bf16[2048,128]{1,0:T(8,128)(2,1)}, bf16[2048,128]{1,0:T(8,128)(2,1)}) custom-call(bf16[32,32,512]{2,1,0:T(8,128)(2,1)S(1)} %all-to-all-done.3.got_ref, bf16[2048,128]{1,0:T(8,128)(2,1)S(1)} %bitcast.6, bf16[2048,128]{1,0:T(8,128)(2,1)S(1)} %bitcast.8, bf16[4,128,128]{2,1,0:T(8,128)(2,1)S(1)} %copy-done.5), custom_call_target="tpu_custom_call" | custom-call | tf_op jit(solution)/shard_map/last_kernel/last_kernel/pallas_call | solution.py:184
  166.6 13.1 %all-to-all-done.4.got_ref = bf16[16,16,8,128]{3,2,1,0:T(8,128)(2,1)S(1)} async-done(((bf16[16,16,8,128]{3,2,1,0:T(8,128)(2,1)}), bf16[16,16,8,128]{3,2,1,0:T(8,128)(2,1)S(1)}, u32[]{:S(2)}, u32[]{:S(2)}) %all-to-all-start.4) | async-done | bytes 524320 | tf_op jit(solution)/shard_map/all_to_all | solution.py:195
  179.7 0.7 sum_kernel.1
Async XLA Ops:
  3.9 13.6 %copy-start.7 = (bf16[4,128,128]{2,1,0:T(8,128)(2,1)S(1)}, bf16[4,128,128]{2,1,0:T(8,128)(2,1)}, u32[]{:S(2)}) copy-start(bf16[4,128,128]{2,1,0:T(8,128)(2,1)} %bwd_ref.2) | copy-start | bytes 393220
  3.9 13.6 %copy-start.8 = (bf16[4,128,128]{2,1,0:T(8,128)(2,1)S(1)}, bf16[4,128,128]{2,1,0:T(8,128)(2,1)}, u32[]{:S(2)}) copy-start(bf16[4,128,128]{2,1,0:T(8,128)(2,1)} %fwd_ref.2) | copy-start | bytes 393220
  4.0 42.5 %all-to-all-start = ((bf16[32,32,512]{2,1,0:T(8,128)(2,1)}), bf16[32,32,512]{2,1,0:T(8,128)(2,1)S(1)}, u32[]{:S(2)}, u32[]{:S(2)}) async-start(bf16[32,32,512]{2,1,0:T(8,128)(2,1)} %first_kernel.1), calls=%async_computation | async-start | bytes 2097152 | tf_op jit(solution)/shard_map/all_to_all | solution.py:195
  46.5 1.7 copy-start
  48.1 5.1 %copy-start.6 = (bf16[4,128,128]{2,1,0:T(8,128)(2,1)S(1)}, bf16[4,128,128]{2,1,0:T(8,128)(2,1)}, u32[]{:S(2)}) copy-start(bf16[4,128,128]{2,1,0:T(8,128)(2,1)} %bwd_ref.1) | copy-start | bytes 393220
  48.1 34.0 %all-to-all-start.1 = ((bf16[32,32,512]{2,1,0:T(8,128)(2,1)}), bf16[32,32,512]{2,1,0:T(8,128)(2,1)S(1)}, u32[]{:S(2)}, u32[]{:S(2)}) async-start(bf16[32,32,512]{2,1,0:T(8,128)(2,1)} %mix_kernel.2), calls=%async_computation.1 | async-start | bytes 2097152 | tf_op jit(solution)/shard_map/all_to_all | solution.py:195
  82.2 1.9 %copy-start.2 = (bf16[32,32,512]{2,1,0:T(8,128)(2,1)}, bf16[32,32,512]{2,1,0:T(8,128)(2,1)S(1)}, u32[]{:S(2)}) copy-start(bf16[32,32,512]{2,1,0:T(8,128)(2,1)S(1)} %all-to-all-done.1.got_ref.got_hbm) | copy-start | bytes 3145732
  84.1 33.9 %all-to-all-start.2 = ((bf16[32,32,512]{2,1,0:T(8,128)(2,1)}), bf16[32,32,512]{2,1,0:T(8,128)(2,1)S(1)}, u32[]{:S(2)}, u32[]{:S(2)}) async-start(bf16[32,32,512]{2,1,0:T(8,128)(2,1)} %get-tuple-element.42), calls=%async_computation.2 | async-start | bytes 2097152 | tf_op jit(solution)/shard_map/all_to_all | solution.py:195
  118.0 1.7 copy-start.1
  119.6 33.9 %all-to-all-start.3 = ((bf16[32,32,512]{2,1,0:T(8,128)(2,1)}), bf16[32,32,512]{2,1,0:T(8,128)(2,1)S(1)}, u32[]{:S(2)}, u32[]{:S(2)}) async-start(bf16[32,32,512]{2,1,0:T(8,128)(2,1)} %mix_kernel.3), calls=%async_computation.3 | async-start | bytes 2097152 | tf_op jit(solution)/shard_map/all_to_all | solution.py:195
  153.5 11.2 %copy-start.5 = (bf16[4,128,128]{2,1,0:T(8,128)(2,1)S(1)}, bf16[4,128,128]{2,1,0:T(8,128)(2,1)}, u32[]{:S(2)}) copy-start(bf16[4,128,128]{2,1,0:T(8,128)(2,1)} %r1_ref.1) | copy-start | bytes 393220
  156.1 8.7 %copy-start.3 = (bf16[512,4,128]{2,1,0:T(4,128)(2,1)S(1)}, bf16[512,4,128]{2,1,0:T(4,128)(2,1)}, u32[]{:S(2)}) copy-start(bf16[512,4,128]{2,1,0:T(4,128)(2,1)} %param.6) | copy-start | bytes 1572868
  156.1 8.6 %copy-start.4 = (bf16[512,4,128]{2,1,0:T(4,128)(2,1)S(1)}, bf16[512,4,128]{2,1,0:T(4,128)(2,1)}, u32[]{:S(2)}) copy-start(bf16[512,4,128]{2,1,0:T(4,128)(2,1)} %param.11) | copy-start | bytes 1572868
  156.1 23.6 %all-to-all-start.4 = ((bf16[16,16,8,128]{3,2,1,0:T(8,128)(2,1)}), bf16[16,16,8,128]{3,2,1,0:T(8,128)(2,1)S(1)}, u32[]{:S(2)}, u32[]{:S(2)}) async-start(bf16[16,16,8,128]{3,2,1,0:T(8,128)(2,1)} %right_grad_kernel.1), calls=%async_computation.4 | async-start | bytes 1048576 | tf_op jit(solution)/shard_map/all_to_all | solution.py:195

commit v3 on v2

--- a/solution.py
+++ b/solution.py
@@ -6,6 +6,7 @@
 from jax.experimental import pallas as pl
 from jax.experimental.pallas import tpu as pltpu
 from jax.sharding import PartitionSpec as P
+
 
 BF = jnp.bfloat16
 F32 = jnp.float32
@@ -116,33 +117,29 @@
     put_rows(out_ref, 16, nn(bwd_ref[...], get_rows(got_ref, 16)) * slope)
 
 
-def grad_of(fwd, bwd, out_ref):
+def grad_of(fwd, bwd, out_ref, first):
     a = nn(one_hot(flat_to_in), fwd).astype(BF)
     b = nn(one_hot(flat_to_out), bwd).astype(BF)
     for m in range(4):
         at = slice(128 * m, 128 * m + 128)
-        out_ref[m] = nt(a[at], b[at]).astype(BF)
+        out_ref[:, first + m, :, :] = nt(a[at], b[at]).reshape(16, 8, 128).astype(BF)
 
 
 def hidden_grad_kernel(h_ref, got_hbm, out_ref, got_ref, sems):
     (got_in,) = fetch(((got_hbm, got_ref),), sems)
     got_in.wait()
-    grad_of(h_ref[...], get_rows(got_ref, 16), out_ref)
-
-
-def left_grads_kernel(one_hbm, three_hbm, l1_ref, l2_ref, one_ref, three_ref, sems):
+    grad_of(h_ref[...], get_rows(got_ref, 16), out_ref, 0)
+
+
+def left_grads_kernel(one_hbm, three_hbm, out_ref, one_ref, three_ref, sems):
     for copy in fetch(((one_hbm, one_ref), (three_hbm, three_ref)), sems):
         copy.wait()
-    grad_of(get_rows(one_ref, 0), get_rows(three_ref, 16), l1_ref)
-    grad_of(get_rows(three_ref, 0), get_rows(one_ref, 16), l2_ref)
-
-
-def right_grad_kernel(got_ref, x_hbm, l1_ref, r2_ref, l2_ref, out_ref, xs_ref, x_ref, sems):
+    grad_of(get_rows(one_ref, 0), get_rows(three_ref, 16), out_ref, 0)
+    grad_of(get_rows(three_ref, 0), get_rows(one_ref, 16), out_ref, 4)
+
+
+def right_grad_kernel(got_ref, x_hbm, out_ref, xs_ref, x_ref, sems):
     (x_in,) = fetch(((x_hbm, x_ref),), sems)
-    for n, ref in enumerate((l1_ref, r2_ref, l2_ref)):
-        for b in range(4):
-            g = ref[b].astype(F32).reshape(16, 8, 128)
-            out_ref[:, 4 * n + 4 + b, :, :] = g.astype(BF)
     d = nn(one_hot(flat_to_out), get_rows(got_ref, 16)).astype(BF)
     x_in.wait()
     xs_ref[...] = x_ref[...].astype(F32)
@@ -162,12 +159,11 @@
     in_ref[...] = (g_ref[...].astype(F32) + s_ref[...]).astype(BF)
 
 
-def sum_kernel(got_ref, r1_ref, l1_ref, r2_ref, l2_ref):
-    for n, ref in enumerate((r1_ref, l1_ref, r2_ref, l2_ref)):
-        total = got_ref[0, 4 * n : 4 * n + 4].astype(F32)
-        for k in range(1, 16):
-            total = total + got_ref[k, 4 * n : 4 * n + 4].astype(F32)
-        ref[...] = total
+def sum_kernel(got_ref, out_ref):
+    total = got_ref[0].astype(F32)
+    for k in range(1, 16):
+        total = total + got_ref[k].astype(F32)
+    out_ref[...] = total
 
 
 ROWS = (2048, 128)
@@ -180,19 +176,44 @@
     args = [pltpu.with_memory_space_constraint(a, pltpu.HBM) if n in far else a for n, a in enumerate(args)]
     outs = [jax.ShapeDtypeStruct(s, d) for s, d in shapes]
     specs = [pl.BlockSpec(memory_space=pltpu.HBM if n in far else pltpu.VMEM) for n in range(len(args))]
-    with jax.named_scope(kernel.__name__):
-        return pl.pallas_call(
-            kernel,
-            out_shape=outs,
-            in_specs=specs,
-            scratch_shapes=scratch,
-            name=kernel.__name__,
-            compiler_params=pltpu.CompilerParams(vmem_limit_bytes=16 << 20),
-        )(*args)
+    return pl.pallas_call(
+        kernel,
+        out_shape=outs,
+        in_specs=specs,
+        scratch_shapes=scratch,
+        compiler_params=pltpu.CompilerParams(vmem_limit_bytes=16 << 20),
+    )(*args)
 
 
 def swap(x, axis):
     return lax.all_to_all(x, axis, 0, 0, tiled=True)
+
+
+def sent(x, mask):
+    return lax.ppermute(x, "dp", [(i, i ^ mask) for i in range(16)])
+
+
+def added(parts):
+    me = lax.axis_index("dp")
+    rest = parts.shape[1:]
+    parts = parts.reshape(2, 4, 2, *rest)
+
+    def near(who):
+        at = (who >> 3, 0, who & 1) + (0,) * len(rest)
+        return lax.dynamic_slice(parts, at, (1, 4, 1, *rest), allow_negative_indices=False).reshape(4, *rest)
+
+    total = near(me).astype(F32)
+    for mask in (8, 1, 9):
+        total = total + sent(near(me ^ mask), mask).astype(F32)
+    half = total.astype(BF)
+
+    def far(who):
+        return lax.dynamic_index_in_dim(half, (who >> 1) & 3, 0, False, allow_negative_indices=False)
+
+    own = lax.dynamic_index_in_dim(total, (me >> 1) & 3, 0, False, allow_negative_indices=False)
+    for mask in (2, 4, 6):
+        own = own + sent(far(me ^ mask), mask).astype(F32)
+    return own
 
 
 def after(first, *values):
@@ -204,7 +225,6 @@
     g = out_grad.reshape(ROWS)
     chunk = ((32, 32, 512), BF)
     square = ((512, 512), BF)
-    grad = ((4, 128, 128), BF)
     (send,) = call(
         first_kernel,
         [chunk],
@@ -233,32 +253,32 @@
     fwd, bwd = call(weights_kernel, [square] * 2, *after(send, left_two, left_one))
     (gr2,) = call(
         hidden_grad_kernel,
-        [grad],
+        [((16, 4, 8, 128), BF)],
         h,
         two,
         scratch=(CHUNK, pltpu.SemaphoreType.DMA((1,))),
         far=(1,),
     )
+    gr2 = added(gr2)
     three, gr2 = lax.optimization_barrier((three, gr2))
     (send,) = call(mix_kernel, [chunk], three, fwd, bwd)
     (three,) = after(send, three)
     four = swap(send, "tensor")
-    gl1, gl2 = call(
+    (left,) = call(
         left_grads_kernel,
-        [grad] * 2,
+        [((16, 8, 8, 128), BF)],
         one,
         three,
         scratch=(CHUNK, CHUNK, pltpu.SemaphoreType.DMA((2,))),
         far=(0, 1),
     )
+    left = added(left)
+    four, left = lax.optimization_barrier((four, left))
     (send,) = call(
         right_grad_kernel,
-        [((16, 16, 8, 128), BF)],
+        [((16, 4, 8, 128), BF)],
         four,
         x,
-        gl1,
-        gr2,
-        gl2,
         scratch=(WIDE_ROWS, HALF_ROWS, pltpu.SemaphoreType.DMA((1,))),
         far=(1,),
     )
@@ -266,8 +286,9 @@
     layer_out, input_grad = call(
         last_kernel, [(ROWS, BF)] * 2, four, x, g, right_one, scratch=(WIDE_ROWS,)
     )
-    grads = call(sum_kernel, [((4, 8, 128), F32)] * 4, sums)
-    return (layer_out.reshape(512, 4, 128), input_grad.reshape(512, 4, 128), *grads)
+    (gr1,) = call(sum_kernel, [((4, 8, 128), F32)], sums)
+    shape = (512, 4, 128)
+    return (layer_out.reshape(shape), input_grad.reshape(shape), gr1, left[:4], gr2, left[4:])
 
 
 def solution(mesh):

time: 181 us -> 186 us (1.028)
  the two profiles are of different devices: /device:TPU:14 before, /device:TPU:4 now
where the time goes in v3:
time: 186 us; the launch traced here: 185 us
  starting transfers between devices  84.2 us (45%)
  waiting for transfers between devices  75.9 us (41%)
  Pallas kernels  22 us (12%)
    all_to_all x5, waiting for transfers between devices, swap(): return lax.all_to_all(x, axis, 0, 0, tiled=True)  61.6 us
    ppermute x12, starting transfers between devices, sent(): return lax.ppermute(x, 'dp', [(i, i ^ mask) for i in range(16)])  42.9 us
    all_to_all x5, starting transfers between devices, swap(): return lax.all_to_all(x, axis, 0, 0, tiled=True)  41.3 us
    pallas_call x12, Pallas kernels, call(): pl.pallas_call(kernel, out_shape=outs, in_specs=specs, scratch_shapes=scr...  22 us
    ppermute x12, waiting for transfers between devices, sent(): return lax.ppermute(x, 'dp', [(i, i ^ mask) for i in range(16)])  14.3 us
  transfers between devices with their start and end apart: 17, of which 9 were waited for; matrix products, arithmetic and copies ran while one was open for 1% of the time, Pallas kernels for 6%

profile of v3, /device:TPU:4, one launch (start us, length us, event | category | flops | bytes accessed | tf_op | source)
XLA Modules:
  0.0 184.6 jit_solution(13418042135784635901)
XLA Ops:
  0.6 3.3 %shard_map.109 = bf16[32,32,512]{2,1,0:T(8,128)(2,1)} custom-call(bf16[2048,128]{1,0:T(8,128)(2,1)} %bitcast.50, bf16[2048,128]{1,0:T(8,128)(2,1)} %bitcast.53, bf16[4,128,128]{2,1,0:T(8,128)(2,1)} %r1_ref.1), custom_call_target="tpu_custom_call" | custom-call | tf_op jit(solution)/shard_map/pallas_call | solution.py:179
  3.9 0.0 copy-start.7
  3.9 0.0 copy-start.8
  4.0 13.6 %all-to-all-start = ((bf16[32,32,512]{2,1,0:T(8,128)(2,1)}), bf16[32,32,512]{2,1,0:T(8,128)(2,1)S(1)}, u32[]{:S(2)}, u32[]{:S(2)}) async-start(bf16[32,32,512]{2,1,0:T(8,128)(2,1)} %shard_map.109), calls=%async_computation | async-start | bytes 2097152 | tf_op jit(solution)/shard_map/all_to_all | solution.py:189
  17.5 0.0 copy-done.7
  17.5 0.0 copy-done.8
  17.6 1.1 shard_map.110
  18.6 27.8 %all-to-all-done.got_ref.one_hbm = bf16[32,32,512]{2,1,0:T(8,128)(2,1)S(1)} async-done(((bf16[32,32,512]{2,1,0:T(8,128)(2,1)}), bf16[32,32,512]{2,1,0:T(8,128)(2,1)S(1)}, u32[]{:S(2)}, u32[]{:S(2)}) %all-to-all-start) | async-done | bytes 1048608 | tf_op jit(solution)/shard_map/all_to_all | solution.py:189
  46.4 0.0 copy-start
  46.4 1.7 shard_map.111
  48.1 0.0 copy-done
  48.1 0.0 copy-start.6
  48.1 5.1 %all-to-all-start.1 = ((bf16[32,32,512]{2,1,0:T(8,128)(2,1)}), bf16[32,32,512]{2,1,0:T(8,128)(2,1)S(1)}, u32[]{:S(2)}, u32[]{:S(2)}) async-start(bf16[32,32,512]{2,1,0:T(8,128)(2,1)} %shard_map.111), calls=%async_computation.1 | async-start | bytes 2097152 | tf_op jit(solution)/shard_map/all_to_all | solution.py:189
  53.3 0.0 copy-done.6
  53.3 1.1 shard_map.112
  54.4 27.8 %all-to-all-done.1.got_ref.got_hbm = bf16[32,32,512]{2,1,0:T(8,128)(2,1)S(1)} async-done(((bf16[32,32,512]{2,1,0:T(8,128)(2,1)}), bf16[32,32,512]{2,1,0:T(8,128)(2,1)S(1)}, u32[]{:S(2)}, u32[]{:S(2)}) %all-to-all-start.1) | async-done | bytes 1048608 | tf_op jit(solution)/shard_map/all_to_all | solution.py:189
  82.2 1.9 %shard_map.113 = (bf16[32,32,512]{2,1,0:T(8,128)(2,1)}, bf16[512,512]{1,0:T(8,128)(2,1)S(1)}) custom-call(bf16[32,32,512]{2,1,0:T(8,128)(2,1)S(1)} %all-to-all-done.1.got_ref.got_hbm, bf16[512,512]{1,0:T(8,128)(2,1)S(1)} %get-tuple-element.36.fwd_ref, bf16[512,512]{1,0:T(8,128)(2,1)S(1)} %get-tuple-element.37.bwd_ref), custom_call_target="tpu_custom_call" | custom-call | tf_op jit(solution)/shard_map/pallas_call | solution.py:179
  84.1 0.0 copy-done.2
  84.1 5.0 %all-to-all-start.2 = ((bf16[32,32,512]{2,1,0:T(8,128)(2,1)}), bf16[32,32,512]{2,1,0:T(8,128)(2,1)S(1)}, u32[]{:S(2)}, u32[]{:S(2)}) async-start(bf16[32,32,512]{2,1,0:T(8,128)(2,1)} %get-tuple-element.38), calls=%async_computation.2 | async-start | bytes 2097152 | tf_op jit(solution)/shard_map/all_to_all | solution.py:189
  89.1 2.2 %shard_map.114 = bf16[16,4,8,128]{3,2,1,0:T(8,128)(2,1)S(1)} custom-call(bf16[512,512]{1,0:T(8,128)(2,1)S(1)} %get-tuple-element.40.h_ref, bf16[32,32,512]{2,1,0:T(8,128)(2,1)} %copy-done.2), custom_call_target="tpu_custom_call" | custom-call | tf_op jit(solution)/shard_map/pallas_call | solution.py:179
  91.3 3.1 %collective-permute-start = (bf16[4,4,8,128]{3,2,1,0:T(8,128)(2,1)S(1)}, bf16[4,4,8,128]{3,2,1,0:T(8,128)(2,1)S(1)}, u32[]{:S(2)}, u32[]{:S(2)}) collective-permute-start(bf16[4,4,8,128]{3,2,1,0:T(8,128)(2,1)S(1)} %get-tuple-element.61), channel_id=1, source_target_pairs={{0,256},{32,288},{64,320},{96,352},{128,384},{160,416},{192,448},{... | collective-permute-start | bytes 98312 | tf_op jit(solution)/shard_map/ppermute | solution.py:193
  94.4 3.8 %collective-permute-start.2 = (bf16[4,4,8,128]{3,2,1,0:T(8,128)(2,1)S(1)}, bf16[4,4,8,128]{3,2,1,0:T(8,128)(2,1)S(1)}, u32[]{:S(2)}, u32[]{:S(2)}) collective-permute-start(bf16[4,4,8,128]{3,2,1,0:T(8,128)(2,1)S(1)} %get-tuple-element.62), channel_id=1, source_target_pairs={{0,288},{32,256},{64,352},{96,320},{128,416},{160,384},{192,480},{... | collective-permute-start | bytes 98312 | tf_op jit(solution)/shard_map/ppermute | solution.py:193
  98.1 2.3 %collective-permute-start.1 = (bf16[4,4,8,128]{3,2,1,0:T(8,128)(2,1)S(1)}, bf16[4,4,8,128]{3,2,1,0:T(8,128)(2,1)S(1)}, u32[]{:S(2)}, u32[]{:S(2)}) collective-permute-start(bf16[4,4,8,128]{3,2,1,0:T(8,128)(2,1)S(1)} %get-tuple-element.63), channel_id=1, source_target_pairs={{0,32},{32,0},{64,96},{96,64},{128,160},{160,128},{192,224},{224,1... | collective-permute-start | bytes 98312 | tf_op jit(solution)/shard_map/ppermute | solution.py:193
  100.5 0.0 collective-permute-done
  100.5 1.1 collective-permute-done.2
  101.6 2.3 %collective-permute-done.1 = bf16[4,4,8,128]{3,2,1,0:T(8,128)(2,1)S(1)} collective-permute-done((bf16[4,4,8,128]{3,2,1,0:T(8,128)(2,1)S(1)}, bf16[4,4,8,128]{3,2,1,0:T(8,128)(2,1)S(1)}, u32[]{:S(2)}, u32[]{:S(2)}) %collective-permute-start.1) | collective-permute-done | bytes 32800 | tf_op jit(solution)/shard_map/ppermute | solution.py:193
  104.0 4.5 %collective-permute-start.3 = (bf16[4,8,128]{2,1,0:T(8,128)(2,1)S(1)}, bf16[4,8,128]{2,1,0:T(8,128)(2,1)S(1)}, u32[]{:S(2)}, u32[]{:S(2)}) collective-permute-start(bf16[4,8,128]{2,1,0:T(8,128)(2,1)S(1)} %get-tuple-element.69), channel_id=1, source_target_pairs={{0,64},{32,96},{64,0},{96,32},{128,192},{160,224},{192,128},{224,1... | collective-permute-start | bytes 24584 | tf_op jit(solution)/shard_map/ppermute | solution.py:193
  108.5 4.8 %collective-permute-start.5 = (bf16[4,8,128]{2,1,0:T(8,128)(2,1)S(1)}, bf16[4,8,128]{2,1,0:T(8,128)(2,1)S(1)}, u32[]{:S(2)}, u32[]{:S(2)}) collective-permute-start(bf16[4,8,128]{2,1,0:T(8,128)(2,1)S(1)} %get-tuple-element.70), channel_id=1, source_target_pairs={{0,192},{32,224},{64,128},{96,160},{128,64},{160,96},{192,0},{224,... | collective-permute-start | bytes 24584 | tf_op jit(solution)/shard_map/ppermute | solution.py:193
  113.3 2.9 %collective-permute-start.4 = (bf16[4,8,128]{2,1,0:T(8,128)(2,1)S(1)}, bf16[4,8,128]{2,1,0:T(8,128)(2,1)S(1)}, u32[]{:S(2)}, u32[]{:S(2)}) collective-permute-start(bf16[4,8,128]{2,1,0:T(8,128)(2,1)S(1)} %get-tuple-element.71), channel_id=1, source_target_pairs={{0,128},{32,160},{64,192},{96,224},{128,0},{160,32},{192,64},{224,... | collective-permute-start | bytes 24584 | tf_op jit(solution)/shard_map/ppermute | solution.py:193
  116.3 1.1 shard_map.115
  117.3 0.0 collective-permute-done.3
  117.3 0.0 collective-permute-done.5
  117.4 5.4 %collective-permute-done.4 = bf16[4,8,128]{2,1,0:T(8,128)(2,1)S(1)} collective-permute-done((bf16[4,8,128]{2,1,0:T(8,128)(2,1)S(1)}, bf16[4,8,128]{2,1,0:T(8,128)(2,1)S(1)}, u32[]{:S(2)}, u32[]{:S(2)}) %collective-permute-start.4) | collective-permute-done | bytes 8224 | tf_op jit(solution)/shard_map/ppermute | solution.py:193
  122.8 0.6 fusion.7
  123.4 0.0 all-to-all-done.2.got_ref.three_hbm
  123.4 1.7 shard_map.116
  125.1 0.0 copy-done.1
  125.1 9.8 %all-to-all-start.3 = ((bf16[32,32,512]{2,1,0:T(8,128)(2,1)}), bf16[32,32,512]{2,1,0:T(8,128)(2,1)S(1)}, u32[]{:S(2)}, u32[]{:S(2)}) async-start(bf16[32,32,512]{2,1,0:T(8,128)(2,1)} %shard_map.116), calls=%async_computation.3 | async-start | bytes 2097152 | tf_op jit(solution)/shard_map/all_to_all | solution.py:189
  134.9 3.2 %shard_map.117 = bf16[16,8,8,128]{3,2,1,0:T(8,128)(2,1)S(1)} custom-call(bf16[32,32,512]{2,1,0:T(8,128)(2,1)} %copy-done, bf16[32,32,512]{2,1,0:T(8,128)(2,1)} %copy-done.1), custom_call_target="tpu_custom_call" | custom-call | tf_op jit(solution)/shard_map/pallas_call | solution.py:179
  138.1 3.1 %collective-permute-start.6 = (bf16[4,8,8,128]{3,2,1,0:T(8,128)(2,1)S(1)}, bf16[4,8,8,128]{3,2,1,0:T(8,128)(2,1)S(1)}, u32[]{:S(2)}, u32[]{:S(2)}) collective-permute-start(bf16[4,8,8,128]{3,2,1,0:T(8,128)(2,1)S(1)} %get-tuple-element.58), channel_id=1, source_target_pairs={{0,256},{32,288},{64,320},{96,352},{128,384},{160,416},{192,448},{... | collective-permute-start | bytes 196616 | tf_op jit(solution)/shard_map/ppermute | solution.py:193
  141.2 3.5 %collective-permute-start.8 = (bf16[4,8,8,128]{3,2,1,0:T(8,128)(2,1)S(1)}, bf16[4,8,8,128]{3,2,1,0:T(8,128)(2,1)S(1)}, u32[]{:S(2)}, u32[]{:S(2)}) collective-permute-start(bf16[4,8,8,128]{3,2,1,0:T(8,128)(2,1)S(1)} %get-tuple-element.59), channel_id=1, source_target_pairs={{0,288},{32,256},{64,352},{96,320},{128,416},{160,384},{192,480},{... | collective-permute-start | bytes 196616 | tf_op jit(solution)/shard_map/ppermute | solution.py:193
  144.7 2.6 %collective-permute-start.7 = (bf16[4,8,8,128]{3,2,1,0:T(8,128)(2,1)S(1)}, bf16[4,8,8,128]{3,2,1,0:T(8,128)(2,1)S(1)}, u32[]{:S(2)}, u32[]{:S(2)}) collective-permute-start(bf16[4,8,8,128]{3,2,1,0:T(8,128)(2,1)S(1)} %get-tuple-element.60), channel_id=1, source_target_pairs={{0,32},{32,0},{64,96},{96,64},{128,160},{160,128},{192,224},{224,1... | collective-permute-start | bytes 196616 | tf_op jit(solution)/shard_map/ppermute | solution.py:193
  147.3 1.3 collective-permute-done.6
  148.6 0.0 collective-permute-done.8
  148.6 2.2 %collective-permute-done.7 = bf16[4,8,8,128]{3,2,1,0:T(8,128)(2,1)S(1)} collective-permute-done((bf16[4,8,8,128]{3,2,1,0:T(8,128)(2,1)S(1)}, bf16[4,8,8,128]{3,2,1,0:T(8,128)(2,1)S(1)}, u32[]{:S(2)}, u32[]{:S(2)}) %collective-permute-start.7) | collective-permute-done | bytes 65568 | tf_op jit(solution)/shard_map/ppermute | solution.py:193
  150.9 2.7 %collective-permute-start.9 = (bf16[8,8,128]{2,1,0:T(8,128)(2,1)S(1)}, bf16[8,8,128]{2,1,0:T(8,128)(2,1)S(1)}, u32[]{:S(2)}, u32[]{:S(2)}) collective-permute-start(bf16[8,8,128]{2,1,0:T(8,128)(2,1)S(1)} %get-tuple-element.64), channel_id=1, source_target_pairs={{0,64},{32,96},{64,0},{96,32},{128,192},{160,224},{192,128},{224,1... | collective-permute-start | bytes 49160 | tf_op jit(solution)/shard_map/ppermute | solution.py:193
  153.6 1.9 %collective-permute-start.11 = (bf16[8,8,128]{2,1,0:T(8,128)(2,1)S(1)}, bf16[8,8,128]{2,1,0:T(8,128)(2,1)S(1)}, u32[]{:S(2)}, u32[]{:S(2)}) collective-permute-start(bf16[8,8,128]{2,1,0:T(8,128)(2,1)S(1)} %get-tuple-element.65), channel_id=1, source_target_pairs={{0,192},{32,224},{64,128},{96,160},{128,64},{160,96},{192,0},{224,... | collective-permute-start | bytes 49160 | tf_op jit(solution)/shard_map/ppermute | solution.py:193
  155.6 7.6 %collective-permute-start.10 = (bf16[8,8,128]{2,1,0:T(8,128)(2,1)S(1)}, bf16[8,8,128]{2,1,0:T(8,128)(2,1)S(1)}, u32[]{:S(2)}, u32[]{:S(2)}) collective-permute-start(bf16[8,8,128]{2,1,0:T(8,128)(2,1)S(1)} %get-tuple-element.66), channel_id=1, source_target_pairs={{0,128},{32,160},{64,192},{96,224},{128,0},{160,32},{192,64},{224,... | collective-permute-start | bytes 49160 | tf_op jit(solution)/shard_map/ppermute | solution.py:193
  163.2 0.0 collective-permute-done.9
  163.2 0.0 collective-permute-done.11
  163.2 1.9 %collective-permute-done.10 = bf16[8,8,128]{2,1,0:T(8,128)(2,1)S(1)} collective-permute-done((bf16[8,8,128]{2,1,0:T(8,128)(2,1)S(1)}, bf16[8,8,128]{2,1,0:T(8,128)(2,1)S(1)}, u32[]{:S(2)}, u32[]{:S(2)}) %collective-permute-start.10) | collective-permute-done | bytes 16416 | tf_op jit(solution)/shard_map/ppermute | solution.py:193
  165.1 0.0 all-to-all-done.3.got_ref
  165.1 0.0 copy-start.3
  165.2 0.0 copy-start.4
  165.2 2.3 %shard_map.119 = bf16[16,4,8,128]{3,2,1,0:T(8,128)(2,1)} custom-call(bf16[32,32,512]{2,1,0:T(8,128)(2,1)S(1)} %all-to-all-done.3.got_ref, bf16[2048,128]{1,0:T(8,128)(2,1)} %bitcast.51), custom_call_target="tpu_custom_call" | custom-call | tf_op jit(solution)/shard_map/pallas_call | solution.py:179
  167.5 0.0 copy-start.5
  167.5 7.9 %all-to-all-start.4 = ((bf16[16,4,8,128]{3,2,1,0:T(8,128)(2,1)}), bf16[16,4,8,128]{3,2,1,0:T(8,128)(2,1)S(1)}, u32[]{:S(2)}, u32[]{:S(2)}) async-start(bf16[16,4,8,128]{3,2,1,0:T(8,128)(2,1)} %shard_map.119), calls=%async_computation.4 | async-start | bytes 262144 | tf_op jit(solution)/shard_map/all_to_all | solution.py:189
  175.4 0.0 copy-done.3
  175.4 0.0 copy-done.4
  175.4 0.0 copy-done.5
  175.4 1.9 %shard_map.118 = (bf16[2048,128]{1,0:T(8,128)(2,1)}, bf16[2048,128]{1,0:T(8,128)(2,1)}) custom-call(bf16[32,32,512]{2,1,0:T(8,128)(2,1)S(1)} %all-to-all-done.3.got_ref, bf16[2048,128]{1,0:T(8,128)(2,1)S(1)} %bitcast.52, bf16[2048,128]{1,0:T(8,128)(2,1)S(1)} %bitcast.54, bf16[4,128,128]{2,1,0:T(8,128)(2,1)S(1)} %copy-done.5), custom_call_target="tpu_custom_call" | custom-call | tf_op jit(solution)/shard_map/pallas_call | solution.py:179
  177.3 0.6 fusion.12
  177.9 6.0 %all-to-all-done.4.got_ref = bf16[16,4,8,128]{3,2,1,0:T(8,128)(2,1)S(1)} async-done(((bf16[16,4,8,128]{3,2,1,0:T(8,128)(2,1)}), bf16[16,4,8,128]{3,2,1,0:T(8,128)(2,1)S(1)}, u32[]{:S(2)}, u32[]{:S(2)}) %all-to-all-start.4) | async-done | bytes 131104 | tf_op jit(solution)/shard_map/all_to_all | solution.py:189
  183.9 0.6 shard_map.120
  (9 shorter events, 0.2 us)
Async XLA Ops:
  3.9 13.6 %copy-start.7 = (bf16[4,128,128]{2,1,0:T(8,128)(2,1)S(1)}, bf16[4,128,128]{2,1,0:T(8,128)(2,1)}, u32[]{:S(2)}) copy-start(bf16[4,128,128]{2,1,0:T(8,128)(2,1)} %bwd_ref.2) | copy-start | bytes 393220
  3.9 13.6 %copy-start.8 = (bf16[4,128,128]{2,1,0:T(8,128)(2,1)S(1)}, bf16[4,128,128]{2,1,0:T(8,128)(2,1)}, u32[]{:S(2)}) copy-start(bf16[4,128,128]{2,1,0:T(8,128)(2,1)} %fwd_ref.2) | copy-start | bytes 393220
  4.0 42.5 %all-to-all-start = ((bf16[32,32,512]{2,1,0:T(8,128)(2,1)}), bf16[32,32,512]{2,1,0:T(8,128)(2,1)S(1)}, u32[]{:S(2)}, u32[]{:S(2)}) async-start(bf16[32,32,512]{2,1,0:T(8,128)(2,1)} %shard_map.109), calls=%async_computation | async-start | bytes 2097152 | tf_op jit(solution)/shard_map/all_to_all | solution.py:189
  46.4 1.7 copy-start
  48.1 5.1 %copy-start.6 = (bf16[4,128,128]{2,1,0:T(8,128)(2,1)S(1)}, bf16[4,128,128]{2,1,0:T(8,128)(2,1)}, u32[]{:S(2)}) copy-start(bf16[4,128,128]{2,1,0:T(8,128)(2,1)} %bwd_ref.1) | copy-start | bytes 393220
  48.1 34.0 %all-to-all-start.1 = ((bf16[32,32,512]{2,1,0:T(8,128)(2,1)}), bf16[32,32,512]{2,1,0:T(8,128)(2,1)S(1)}, u32[]{:S(2)}, u32[]{:S(2)}) async-start(bf16[32,32,512]{2,1,0:T(8,128)(2,1)} %shard_map.111), calls=%async_computation.1 | async-start | bytes 2097152 | tf_op jit(solution)/shard_map/all_to_all | solution.py:189
  82.2 1.9 %copy-start.2 = (bf16[32,32,512]{2,1,0:T(8,128)(2,1)}, bf16[32,32,512]{2,1,0:T(8,128)(2,1)S(1)}, u32[]{:S(2)}) copy-start(bf16[32,32,512]{2,1,0:T(8,128)(2,1)S(1)} %all-to-all-done.1.got_ref.got_hbm) | copy-start | bytes 3145732
  84.1 39.3 %all-to-all-start.2 = ((bf16[32,32,512]{2,1,0:T(8,128)(2,1)}), bf16[32,32,512]{2,1,0:T(8,128)(2,1)S(1)}, u32[]{:S(2)}, u32[]{:S(2)}) async-start(bf16[32,32,512]{2,1,0:T(8,128)(2,1)} %get-tuple-element.38), calls=%async_computation.2 | async-start | bytes 2097152 | tf_op jit(solution)/shard_map/all_to_all | solution.py:189
  91.3 9.2 %collective-permute-start = (bf16[4,4,8,128]{3,2,1,0:T(8,128)(2,1)S(1)}, bf16[4,4,8,128]{3,2,1,0:T(8,128)(2,1)S(1)}, u32[]{:S(2)}, u32[]{:S(2)}) collective-permute-start(bf16[4,4,8,128]{3,2,1,0:T(8,128)(2,1)S(1)} %get-tuple-element.61), channel_id=1, source_target_pairs={{0,256},{32,288},{64,320},{96,352},{128,384},{160,416},{192,448},{... | collective-permute-start | bytes 98312 | tf_op jit(solution)/shard_map/ppermute | solution.py:193
  94.4 7.3 %collective-permute-start.2 = (bf16[4,4,8,128]{3,2,1,0:T(8,128)(2,1)S(1)}, bf16[4,4,8,128]{3,2,1,0:T(8,128)(2,1)S(1)}, u32[]{:S(2)}, u32[]{:S(2)}) collective-permute-start(bf16[4,4,8,128]{3,2,1,0:T(8,128)(2,1)S(1)} %get-tuple-element.62), channel_id=1, source_target_pairs={{0,288},{32,256},{64,352},{96,320},{128,416},{160,384},{192,480},{... | collective-permute-start | bytes 98312 | tf_op jit(solution)/shard_map/ppermute | solution.py:193
  98.1 5.8 %collective-permute-start.1 = (bf16[4,4,8,128]{3,2,1,0:T(8,128)(2,1)S(1)}, bf16[4,4,8,128]{3,2,1,0:T(8,128)(2,1)S(1)}, u32[]{:S(2)}, u32[]{:S(2)}) collective-permute-start(bf16[4,4,8,128]{3,2,1,0:T(8,128)(2,1)S(1)} %get-tuple-element.63), channel_id=1, source_target_pairs={{0,32},{32,0},{64,96},{96,64},{128,160},{160,128},{192,224},{224,1... | collective-permute-start | bytes 98312 | tf_op jit(solution)/shard_map/ppermute | solution.py:193
  104.0 13.3 %collective-permute-start.3 = (bf16[4,8,128]{2,1,0:T(8,128)(2,1)S(1)}, bf16[4,8,128]{2,1,0:T(8,128)(2,1)S(1)}, u32[]{:S(2)}, u32[]{:S(2)}) collective-permute-start(bf16[4,8,128]{2,1,0:T(8,128)(2,1)S(1)} %get-tuple-element.69), channel_id=1, source_target_pairs={{0,64},{32,96},{64,0},{96,32},{128,192},{160,224},{192,128},{224,1... | collective-permute-start | bytes 24584 | tf_op jit(solution)/shard_map/ppermute | solution.py:193
  108.5 8.8 %collective-permute-start.5 = (bf16[4,8,128]{2,1,0:T(8,128)(2,1)S(1)}, bf16[4,8,128]{2,1,0:T(8,128)(2,1)S(1)}, u32[]{:S(2)}, u32[]{:S(2)}) collective-permute-start(bf16[4,8,128]{2,1,0:T(8,128)(2,1)S(1)} %get-tuple-element.70), channel_id=1, source_target_pairs={{0,192},{32,224},{64,128},{96,160},{128,64},{160,96},{192,0},{224,... | collective-permute-start | bytes 24584 | tf_op jit(solution)/shard_map/ppermute | solution.py:193
  113.3 9.5 %collective-permute-start.4 = (bf16[4,8,128]{2,1,0:T(8,128)(2,1)S(1)}, bf16[4,8,128]{2,1,0:T(8,128)(2,1)S(1)}, u32[]{:S(2)}, u32[]{:S(2)}) collective-permute-start(bf16[4,8,128]{2,1,0:T(8,128)(2,1)S(1)} %get-tuple-element.71), channel_id=1, source_target_pairs={{0,128},{32,160},{64,192},{96,224},{128,0},{160,32},{192,64},{224,... | collective-permute-start | bytes 24584 | tf_op jit(solution)/shard_map/ppermute | solution.py:193
  123.4 1.7 copy-start.1
  125.1 40.1 %all-to-all-start.3 = ((bf16[32,32,512]{2,1,0:T(8,128)(2,1)}), bf16[32,32,512]{2,1,0:T(8,128)(2,1)S(1)}, u32[]{:S(2)}, u32[]{:S(2)}) async-start(bf16[32,32,512]{2,1,0:T(8,128)(2,1)} %shard_map.116), calls=%async_computation.3 | async-start | bytes 2097152 | tf_op jit(solution)/shard_map/all_to_all | solution.py:189
  138.1 10.5 %collective-permute-start.6 = (bf16[4,8,8,128]{3,2,1,0:T(8,128)(2,1)S(1)}, bf16[4,8,8,128]{3,2,1,0:T(8,128)(2,1)S(1)}, u32[]{:S(2)}, u32[]{:S(2)}) collective-permute-start(bf16[4,8,8,128]{3,2,1,0:T(8,128)(2,1)S(1)} %get-tuple-element.58), channel_id=1, source_target_pairs={{0,256},{32,288},{64,320},{96,352},{128,384},{160,416},{192,448},{... | collective-permute-start | bytes 196616 | tf_op jit(solution)/shard_map/ppermute | solution.py:193
  141.2 7.4 %collective-permute-start.8 = (bf16[4,8,8,128]{3,2,1,0:T(8,128)(2,1)S(1)}, bf16[4,8,8,128]{3,2,1,0:T(8,128)(2,1)S(1)}, u32[]{:S(2)}, u32[]{:S(2)}) collective-permute-start(bf16[4,8,8,128]{3,2,1,0:T(8,128)(2,1)S(1)} %get-tuple-element.59), channel_id=1, source_target_pairs={{0,288},{32,256},{64,352},{96,320},{128,416},{160,384},{192,480},{... | collective-permute-start | bytes 196616 | tf_op jit(solution)/shard_map/ppermute | solution.py:193
  144.7 6.2 %collective-permute-start.7 = (bf16[4,8,8,128]{3,2,1,0:T(8,128)(2,1)S(1)}, bf16[4,8,8,128]{3,2,1,0:T(8,128)(2,1)S(1)}, u32[]{:S(2)}, u32[]{:S(2)}) collective-permute-start(bf16[4,8,8,128]{3,2,1,0:T(8,128)(2,1)S(1)} %get-tuple-element.60), channel_id=1, source_target_pairs={{0,32},{32,0},{64,96},{96,64},{128,160},{160,128},{192,224},{224,1... | collective-permute-start | bytes 196616 | tf_op jit(solution)/shard_map/ppermute | solution.py:193
  150.9 12.2 %collective-permute-start.9 = (bf16[8,8,128]{2,1,0:T(8,128)(2,1)S(1)}, bf16[8,8,128]{2,1,0:T(8,128)(2,1)S(1)}, u32[]{:S(2)}, u32[]{:S(2)}) collective-permute-start(bf16[8,8,128]{2,1,0:T(8,128)(2,1)S(1)} %get-tuple-element.64), channel_id=1, source_target_pairs={{0,64},{32,96},{64,0},{96,32},{128,192},{160,224},{192,128},{224,1... | collective-permute-start | bytes 49160 | tf_op jit(solution)/shard_map/ppermute | solution.py:193
  153.6 9.5 %collective-permute-start.11 = (bf16[8,8,128]{2,1,0:T(8,128)(2,1)S(1)}, bf16[8,8,128]{2,1,0:T(8,128)(2,1)S(1)}, u32[]{:S(2)}, u32[]{:S(2)}) collective-permute-start(bf16[8,8,128]{2,1,0:T(8,128)(2,1)S(1)} %get-tuple-element.65), channel_id=1, source_target_pairs={{0,192},{32,224},{64,128},{96,160},{128,64},{160,96},{192,0},{224,... | collective-permute-start | bytes 49160 | tf_op jit(solution)/shard_map/ppermute | solution.py:193
  155.6 9.5 %collective-permute-start.10 = (bf16[8,8,128]{2,1,0:T(8,128)(2,1)S(1)}, bf16[8,8,128]{2,1,0:T(8,128)(2,1)S(1)}, u32[]{:S(2)}, u32[]{:S(2)}) collective-permute-start(bf16[8,8,128]{2,1,0:T(8,128)(2,1)S(1)} %get-tuple-element.66), channel_id=1, source_target_pairs={{0,128},{32,160},{64,192},{96,224},{128,0},{160,32},{192,64},{224,... | collective-permute-start | bytes 49160 | tf_op jit(solution)/shard_map/ppermute | solution.py:193
  165.1 10.2 %copy-start.3 = (bf16[512,4,128]{2,1,0:T(4,128)(2,1)S(1)}, bf16[512,4,128]{2,1,0:T(4,128)(2,1)}, u32[]{:S(2)}) copy-start(bf16[512,4,128]{2,1,0:T(4,128)(2,1)} %param.6) | copy-start | bytes 1572868
  165.2 10.2 %copy-start.4 = (bf16[512,4,128]{2,1,0:T(4,128)(2,1)S(1)}, bf16[512,4,128]{2,1,0:T(4,128)(2,1)}, u32[]{:S(2)}) copy-start(bf16[512,4,128]{2,1,0:T(4,128)(2,1)} %param.11) | copy-start | bytes 1572868
  167.5 7.9 %copy-start.5 = (bf16[4,128,128]{2,1,0:T(8,128)(2,1)S(1)}, bf16[4,128,128]{2,1,0:T(8,128)(2,1)}, u32[]{:S(2)}) copy-start(bf16[4,128,128]{2,1,0:T(8,128)(2,1)} %r1_ref.1) | copy-start | bytes 393220
  167.5 16.4 %all-to-all-start.4 = ((bf16[16,4,8,128]{3,2,1,0:T(8,128)(2,1)}), bf16[16,4,8,128]{3,2,1,0:T(8,128)(2,1)S(1)}, u32[]{:S(2)}, u32[]{:S(2)}) async-start(bf16[16,4,8,128]{3,2,1,0:T(8,128)(2,1)} %shard_map.119), calls=%async_computation.4 | async-start | bytes 262144 | tf_op jit(solution)/shard_map/all_to_all | solution.py:189

commit v4 on v3

--- a/solution.py
+++ b/solution.py
@@ -193,26 +193,35 @@
     return lax.ppermute(x, "dp", [(i, i ^ mask) for i in range(16)])
 
 
-def added(parts):
+def added_near(parts):
     me = lax.axis_index("dp")
     rest = parts.shape[1:]
     parts = parts.reshape(2, 4, 2, *rest)
 
-    def near(who):
+    def of(who):
         at = (who >> 3, 0, who & 1) + (0,) * len(rest)
-        return lax.dynamic_slice(parts, at, (1, 4, 1, *rest), allow_negative_indices=False).reshape(4, *rest)
-
-    total = near(me).astype(F32)
+        return lax.dynamic_slice(
+            parts, at, (1, 4, 1, *rest), allow_negative_indices=False
+        ).reshape(4, *rest)
+
+    total = of(me).astype(F32)
     for mask in (8, 1, 9):
-        total = total + sent(near(me ^ mask), mask).astype(F32)
+        total = total + sent(of(me ^ mask), mask).astype(F32)
+    return total
+
+
+def added_far(total):
+    me = lax.axis_index("dp")
+
+    def of(x, who):
+        return lax.dynamic_index_in_dim(
+            x, (who >> 1) & 3, 0, False, allow_negative_indices=False
+        )
+
     half = total.astype(BF)
-
-    def far(who):
-        return lax.dynamic_index_in_dim(half, (who >> 1) & 3, 0, False, allow_negative_indices=False)
-
-    own = lax.dynamic_index_in_dim(total, (me >> 1) & 3, 0, False, allow_negative_indices=False)
+    own = of(total, me)
     for mask in (2, 4, 6):
-        own = own + sent(far(me ^ mask), mask).astype(F32)
+        own = own + sent(of(half, me ^ mask), mask).astype(F32)
     return own
 
 
@@ -259,7 +268,7 @@
         scratch=(CHUNK, pltpu.SemaphoreType.DMA((1,))),
         far=(1,),
     )
-    gr2 = added(gr2)
+    gr2 = added_near(gr2)
     three, gr2 = lax.optimization_barrier((three, gr2))
     (send,) = call(mix_kernel, [chunk], three, fwd, bwd)
     (three,) = after(send, three)
@@ -272,8 +281,9 @@
         scratch=(CHUNK, CHUNK, pltpu.SemaphoreType.DMA((2,))),
         far=(0, 1),
     )
-    left = added(left)
-    four, left = lax.optimization_barrier((four, left))
+    left = added_near(left)
+    sums = added_far(jnp.concatenate((gr2, left), axis=1))
+    four, sums = lax.optimization_barrier((four, sums))
     (send,) = call(
         right_grad_kernel,
         [((16, 4, 8, 128), BF)],
@@ -282,13 +292,13 @@
         scratch=(WIDE_ROWS, HALF_ROWS, pltpu.SemaphoreType.DMA((1,))),
         far=(1,),
     )
-    sums = swap(send, "dp")
+    got = swap(send, "dp")
     layer_out, input_grad = call(
         last_kernel, [(ROWS, BF)] * 2, four, x, g, right_one, scratch=(WIDE_ROWS,)
     )
-    (gr1,) = call(sum_kernel, [((4, 8, 128), F32)], sums)
+    (gr1,) = call(sum_kernel, [((4, 8, 128), F32)], got)
     shape = (512, 4, 128)
-    return (layer_out.reshape(shape), input_grad.reshape(shape), gr1, left[:4], gr2, left[4:])
+    return (layer_out.reshape(shape), input_grad.reshape(shape), gr1, sums[4:8], sums[:4], sums[8:])
 
 
 def solution(mesh):

time: 186 us -> 176 us (0.946)
  starting transfers between devices: 84.2 us -> 63.1 us
  waiting for transfers between devices: 75.9 us -> 88.5 us
    all_to_all x5, waiting for transfers between devices: 61.6 us -> 75.6 us  [swap(): return lax.all_to_all(x, axis, 0, 0, tiled=True)]
    ppermute x12 -> x9, starting transfers between devices: 42.9 us -> 30.6 us  [sent(): return lax.ppermute(x, 'dp', [(i, i ^ mask) for i in range(16)])]
    all_to_all x5, starting transfers between devices: 41.3 us -> 32.5 us  [swap(): return lax.all_to_all(x, axis, 0, 0, tiled=True)]
    ppermute x12 -> x9, waiting for transfers between devices: 14.3 us -> 12.8 us  [sent(): return lax.ppermute(x, 'dp', [(i, i ^ mask) for i in range(16)])]
  transfers between devices with their start and end apart: 17 -> 14, of which waited for: 9 -> 9; matrix products, arithmetic and copies ran while one was open for 1% -> 0% of each run, Pallas kernels for 6% -> 6%
where the time goes in v4:
time: 176 us; the launch traced here: 175 us
  waiting for transfers between devices  88.5 us (50%)
  starting transfers between devices  63.1 us (36%)
  Pallas kernels  21.9 us (12%)
    all_to_all x5, waiting for transfers between devices, swap(): return lax.all_to_all(x, axis, 0, 0, tiled=True)  75.6 us
    all_to_all x5, starting transfers between devices, swap(): return lax.all_to_all(x, axis, 0, 0, tiled=True)  32.5 us
    ppermute x9, starting transfers between devices, sent(): return lax.ppermute(x, 'dp', [(i, i ^ mask) for i in range(16)])  30.6 us
    pallas_call x12, Pallas kernels, call(): pl.pallas_call(kernel, out_shape=outs, in_specs=specs, scratch_shapes=scr...  21.9 us
    ppermute x9, waiting for transfers between devices, sent(): return lax.ppermute(x, 'dp', [(i, i ^ mask) for i in range(16)])  12.8 us
  transfers between devices with their start and end apart: 14, of which 9 were waited for; matrix products, arithmetic and copies ran while one was open for 0% of the time, Pallas kernels for 6%

profile of v4, /device:TPU:4, one launch (start us, length us, event | category | flops | bytes accessed | tf_op | source)
XLA Modules:
  0.0 175.2 jit_solution(11972590464931125815)
XLA Ops:
  0.6 3.3 %shard_map.109 = bf16[32,32,512]{2,1,0:T(8,128)(2,1)} custom-call(bf16[2048,128]{1,0:T(8,128)(2,1)} %bitcast.40, bf16[2048,128]{1,0:T(8,128)(2,1)} %bitcast.43, bf16[4,128,128]{2,1,0:T(8,128)(2,1)} %r1_ref.1), custom_call_target="tpu_custom_call" | custom-call | tf_op jit(solution)/shard_map/pallas_call | solution.py:179
  3.9 0.0 copy-start.7
  3.9 0.0 copy-start.8
  3.9 13.6 %all-to-all-start = ((bf16[32,32,512]{2,1,0:T(8,128)(2,1)}), bf16[32,32,512]{2,1,0:T(8,128)(2,1)S(1)}, u32[]{:S(2)}, u32[]{:S(2)}) async-start(bf16[32,32,512]{2,1,0:T(8,128)(2,1)} %shard_map.109), calls=%async_computation | async-start | bytes 2097152 | tf_op jit(solution)/shard_map/all_to_all | solution.py:189
  17.5 0.0 copy-done.7
  17.5 0.0 copy-done.8
  17.5 1.1 shard_map.110
  18.6 27.8 %all-to-all-done.got_ref.one_hbm = bf16[32,32,512]{2,1,0:T(8,128)(2,1)S(1)} async-done(((bf16[32,32,512]{2,1,0:T(8,128)(2,1)}), bf16[32,32,512]{2,1,0:T(8,128)(2,1)S(1)}, u32[]{:S(2)}, u32[]{:S(2)}) %all-to-all-start) | async-done | bytes 1048608 | tf_op jit(solution)/shard_map/all_to_all | solution.py:189
  46.4 0.0 copy-start
  46.4 1.7 shard_map.111
  48.1 0.0 copy-done
  48.1 0.0 copy-start.6
  48.1 5.1 %all-to-all-start.1 = ((bf16[32,32,512]{2,1,0:T(8,128)(2,1)}), bf16[32,32,512]{2,1,0:T(8,128)(2,1)S(1)}, u32[]{:S(2)}, u32[]{:S(2)}) async-start(bf16[32,32,512]{2,1,0:T(8,128)(2,1)} %shard_map.111), calls=%async_computation.1 | async-start | bytes 2097152 | tf_op jit(solution)/shard_map/all_to_all | solution.py:189
  53.2 0.0 copy-done.6
  53.2 1.1 shard_map.112
  54.3 27.8 %all-to-all-done.1.got_ref.got_hbm = bf16[32,32,512]{2,1,0:T(8,128)(2,1)S(1)} async-done(((bf16[32,32,512]{2,1,0:T(8,128)(2,1)}), bf16[32,32,512]{2,1,0:T(8,128)(2,1)S(1)}, u32[]{:S(2)}, u32[]{:S(2)}) %all-to-all-start.1) | async-done | bytes 1048608 | tf_op jit(solution)/shard_map/all_to_all | solution.py:189
  82.1 0.0 copy-start.2
  82.1 1.9 %shard_map.113 = (bf16[32,32,512]{2,1,0:T(8,128)(2,1)}, bf16[512,512]{1,0:T(8,128)(2,1)S(1)}) custom-call(bf16[32,32,512]{2,1,0:T(8,128)(2,1)S(1)} %all-to-all-done.1.got_ref.got_hbm, bf16[512,512]{1,0:T(8,128)(2,1)S(1)} %get-tuple-element.36.fwd_ref, bf16[512,512]{1,0:T(8,128)(2,1)S(1)} %get-tuple-element.37.bwd_ref), custom_call_target="tpu_custom_call" | custom-call | tf_op jit(solution)/shard_map/pallas_call | solution.py:179
  84.0 0.0 copy-done.2
  84.0 5.0 %all-to-all-start.2 = ((bf16[32,32,512]{2,1,0:T(8,128)(2,1)}), bf16[32,32,512]{2,1,0:T(8,128)(2,1)S(1)}, u32[]{:S(2)}, u32[]{:S(2)}) async-start(bf16[32,32,512]{2,1,0:T(8,128)(2,1)} %get-tuple-element.38), calls=%async_computation.2 | async-start | bytes 2097152 | tf_op jit(solution)/shard_map/all_to_all | solution.py:189
  89.0 2.1 %shard_map.114 = bf16[16,4,8,128]{3,2,1,0:T(8,128)(2,1)S(1)} custom-call(bf16[512,512]{1,0:T(8,128)(2,1)S(1)} %get-tuple-element.40.h_ref, bf16[32,32,512]{2,1,0:T(8,128)(2,1)} %copy-done.2), custom_call_target="tpu_custom_call" | custom-call | tf_op jit(solution)/shard_map/pallas_call | solution.py:179
  91.2 3.1 %collective-permute-start = (bf16[4,4,8,128]{3,2,1,0:T(8,128)(2,1)S(1)}, bf16[4,4,8,128]{3,2,1,0:T(8,128)(2,1)S(1)}, u32[]{:S(2)}, u32[]{:S(2)}) collective-permute-start(bf16[4,4,8,128]{3,2,1,0:T(8,128)(2,1)S(1)} %get-tuple-element.57), channel_id=1, source_target_pairs={{0,256},{32,288},{64,320},{96,352},{128,384},{160,416},{192,448},{... | collective-permute-start | bytes 98312 | tf_op jit(solution)/shard_map/ppermute | solution.py:193
  94.3 3.8 %collective-permute-start.2 = (bf16[4,4,8,128]{3,2,1,0:T(8,128)(2,1)S(1)}, bf16[4,4,8,128]{3,2,1,0:T(8,128)(2,1)S(1)}, u32[]{:S(2)}, u32[]{:S(2)}) collective-permute-start(bf16[4,4,8,128]{3,2,1,0:T(8,128)(2,1)S(1)} %get-tuple-element.58), channel_id=1, source_target_pairs={{0,288},{32,256},{64,352},{96,320},{128,416},{160,384},{192,480},{... | collective-permute-start | bytes 98312 | tf_op jit(solution)/shard_map/ppermute | solution.py:193
  98.1 2.3 %collective-permute-start.1 = (bf16[4,4,8,128]{3,2,1,0:T(8,128)(2,1)S(1)}, bf16[4,4,8,128]{3,2,1,0:T(8,128)(2,1)S(1)}, u32[]{:S(2)}, u32[]{:S(2)}) collective-permute-start(bf16[4,4,8,128]{3,2,1,0:T(8,128)(2,1)S(1)} %get-tuple-element.59), channel_id=1, source_target_pairs={{0,32},{32,0},{64,96},{96,64},{128,160},{160,128},{192,224},{224,1... | collective-permute-start | bytes 98312 | tf_op jit(solution)/shard_map/ppermute | solution.py:193
  100.4 1.1 shard_map.115
  101.5 0.0 collective-permute-done
  101.5 0.0 collective-permute-done.2
  101.6 2.3 %collective-permute-done.1 = bf16[4,4,8,128]{3,2,1,0:T(8,128)(2,1)S(1)} collective-permute-done((bf16[4,4,8,128]{3,2,1,0:T(8,128)(2,1)S(1)}, bf16[4,4,8,128]{3,2,1,0:T(8,128)(2,1)S(1)}, u32[]{:S(2)}, u32[]{:S(2)}) %collective-permute-start.1) | collective-permute-done | bytes 32800 | tf_op jit(solution)/shard_map/ppermute | solution.py:193
  103.9 14.0 %all-to-all-done.2.got_ref.three_hbm = bf16[32,32,512]{2,1,0:T(8,128)(2,1)S(1)} async-done(((bf16[32,32,512]{2,1,0:T(8,128)(2,1)}), bf16[32,32,512]{2,1,0:T(8,128)(2,1)S(1)}, u32[]{:S(2)}, u32[]{:S(2)}) %all-to-all-start.2) | async-done | bytes 1048608 | tf_op jit(solution)/shard_map/all_to_all | solution.py:189
  117.9 0.0 copy-start.1
  117.9 1.7 shard_map.116
  119.6 0.0 copy-done.1
  119.6 5.0 %all-to-all-start.3 = ((bf16[32,32,512]{2,1,0:T(8,128)(2,1)}), bf16[32,32,512]{2,1,0:T(8,128)(2,1)S(1)}, u32[]{:S(2)}, u32[]{:S(2)}) async-start(bf16[32,32,512]{2,1,0:T(8,128)(2,1)} %shard_map.116), calls=%async_computation.3 | async-start | bytes 2097152 | tf_op jit(solution)/shard_map/all_to_all | solution.py:189
  124.6 3.2 %shard_map.117 = bf16[16,8,8,128]{3,2,1,0:T(8,128)(2,1)S(1)} custom-call(bf16[32,32,512]{2,1,0:T(8,128)(2,1)} %copy-done, bf16[32,32,512]{2,1,0:T(8,128)(2,1)} %copy-done.1), custom_call_target="tpu_custom_call" | custom-call | tf_op jit(solution)/shard_map/pallas_call | solution.py:179
  127.8 3.1 %collective-permute-start.3 = (bf16[4,8,8,128]{3,2,1,0:T(8,128)(2,1)S(1)}, bf16[4,8,8,128]{3,2,1,0:T(8,128)(2,1)S(1)}, u32[]{:S(2)}, u32[]{:S(2)}) collective-permute-start(bf16[4,8,8,128]{3,2,1,0:T(8,128)(2,1)S(1)} %get-tuple-element.54), channel_id=1, source_target_pairs={{0,256},{32,288},{64,320},{96,352},{128,384},{160,416},{192,448},{... | collective-permute-start | bytes 196616 | tf_op jit(solution)/shard_map/ppermute | solution.py:193
  130.9 3.8 %collective-permute-start.5 = (bf16[4,8,8,128]{3,2,1,0:T(8,128)(2,1)S(1)}, bf16[4,8,8,128]{3,2,1,0:T(8,128)(2,1)S(1)}, u32[]{:S(2)}, u32[]{:S(2)}) collective-permute-start(bf16[4,8,8,128]{3,2,1,0:T(8,128)(2,1)S(1)} %get-tuple-element.55), channel_id=1, source_target_pairs={{0,288},{32,256},{64,352},{96,320},{128,416},{160,384},{192,480},{... | collective-permute-start | bytes 196616 | tf_op jit(solution)/shard_map/ppermute | solution.py:193
  134.7 2.3 %collective-permute-start.4 = (bf16[4,8,8,128]{3,2,1,0:T(8,128)(2,1)S(1)}, bf16[4,8,8,128]{3,2,1,0:T(8,128)(2,1)S(1)}, u32[]{:S(2)}, u32[]{:S(2)}) collective-permute-start(bf16[4,8,8,128]{3,2,1,0:T(8,128)(2,1)S(1)} %get-tuple-element.56), channel_id=1, source_target_pairs={{0,32},{32,0},{64,96},{96,64},{128,160},{160,128},{192,224},{224,1... | collective-permute-start | bytes 196616 | tf_op jit(solution)/shard_map/ppermute | solution.py:193
  137.0 1.3 collective-permute-done.3
  138.3 0.0 collective-permute-done.5
  138.3 2.5 %collective-permute-done.4 = bf16[4,8,8,128]{3,2,1,0:T(8,128)(2,1)S(1)} collective-permute-done((bf16[4,8,8,128]{3,2,1,0:T(8,128)(2,1)S(1)}, bf16[4,8,8,128]{3,2,1,0:T(8,128)(2,1)S(1)}, u32[]{:S(2)}, u32[]{:S(2)}) %collective-permute-start.4) | collective-permute-done | bytes 65568 | tf_op jit(solution)/shard_map/ppermute | solution.py:193
  140.9 4.5 %collective-permute-start.6 = (bf16[12,8,128]{2,1,0:T(8,128)(2,1)S(1)}, bf16[12,8,128]{2,1,0:T(8,128)(2,1)S(1)}, u32[]{:S(2)}, u32[]{:S(2)}) collective-permute-start(bf16[12,8,128]{2,1,0:T(8,128)(2,1)S(1)} %get-tuple-element.60), channel_id=1, source_target_pairs={{0,64},{32,96},{64,0},{96,32},{128,192},{160,224},{192,128},{224,1... | collective-permute-start | bytes 73736 | tf_op jit(solution)/shard_map/ppermute | solution.py:193
  145.4 4.8 %collective-permute-start.8 = (bf16[12,8,128]{2,1,0:T(8,128)(2,1)S(1)}, bf16[12,8,128]{2,1,0:T(8,128)(2,1)S(1)}, u32[]{:S(2)}, u32[]{:S(2)}) collective-permute-start(bf16[12,8,128]{2,1,0:T(8,128)(2,1)S(1)} %get-tuple-element.61), channel_id=1, source_target_pairs={{0,192},{32,224},{64,128},{96,160},{128,64},{160,96},{192,0},{224,... | collective-permute-start | bytes 73736 | tf_op jit(solution)/shard_map/ppermute | solution.py:193
  150.2 2.9 %collective-permute-start.7 = (bf16[12,8,128]{2,1,0:T(8,128)(2,1)S(1)}, bf16[12,8,128]{2,1,0:T(8,128)(2,1)S(1)}, u32[]{:S(2)}, u32[]{:S(2)}) collective-permute-start(bf16[12,8,128]{2,1,0:T(8,128)(2,1)S(1)} %get-tuple-element.62), channel_id=1, source_target_pairs={{0,128},{32,160},{64,192},{96,224},{128,0},{160,32},{192,64},{224,... | collective-permute-start | bytes 73736 | tf_op jit(solution)/shard_map/ppermute | solution.py:193
  153.2 0.0 collective-permute-done.6
  153.2 0.1 collective-permute-done.8
  153.2 6.6 %collective-permute-done.7 = bf16[12,8,128]{2,1,0:T(8,128)(2,1)S(1)} collective-permute-done((bf16[12,8,128]{2,1,0:T(8,128)(2,1)S(1)}, bf16[12,8,128]{2,1,0:T(8,128)(2,1)S(1)}, u32[]{:S(2)}, u32[]{:S(2)}) %collective-permute-start.7) | collective-permute-done | bytes 24608 | tf_op jit(solution)/shard_map/ppermute | solution.py:193
  159.9 0.0 all-to-all-done.3.got_ref
  159.9 0.0 copy-start.3
  159.9 0.0 copy-start.4
  159.9 2.3 %shard_map.119 = bf16[16,4,8,128]{3,2,1,0:T(8,128)(2,1)} custom-call(bf16[32,32,512]{2,1,0:T(8,128)(2,1)S(1)} %all-to-all-done.3.got_ref, bf16[2048,128]{1,0:T(8,128)(2,1)} %bitcast.41), custom_call_target="tpu_custom_call" | custom-call | tf_op jit(solution)/shard_map/pallas_call | solution.py:179
  162.2 0.0 copy-start.5
  162.2 3.8 %all-to-all-start.4 = ((bf16[16,4,8,128]{3,2,1,0:T(8,128)(2,1)}), bf16[16,4,8,128]{3,2,1,0:T(8,128)(2,1)S(1)}, u32[]{:S(2)}, u32[]{:S(2)}) async-start(bf16[16,4,8,128]{3,2,1,0:T(8,128)(2,1)} %shard_map.119), calls=%async_computation.4 | async-start | bytes 262144 | tf_op jit(solution)/shard_map/all_to_all | solution.py:189
  166.0 0.0 copy-done.3
  166.0 0.0 copy-done.4
  166.0 0.0 copy-done.5
  166.1 1.9 %shard_map.118 = (bf16[2048,128]{1,0:T(8,128)(2,1)}, bf16[2048,128]{1,0:T(8,128)(2,1)}) custom-call(bf16[32,32,512]{2,1,0:T(8,128)(2,1)S(1)} %all-to-all-done.3.got_ref, bf16[2048,128]{1,0:T(8,128)(2,1)S(1)} %bitcast.42, bf16[2048,128]{1,0:T(8,128)(2,1)S(1)} %bitcast.44, bf16[4,128,128]{2,1,0:T(8,128)(2,1)S(1)} %copy-done.5), custom_call_target="tpu_custom_call" | custom-call | tf_op jit(solution)/shard_map/pallas_call | solution.py:179
  168.0 0.6 fusion.10
  168.6 6.0 %all-to-all-done.4.got_ref = bf16[16,4,8,128]{3,2,1,0:T(8,128)(2,1)S(1)} async-done(((bf16[16,4,8,128]{3,2,1,0:T(8,128)(2,1)}), bf16[16,4,8,128]{3,2,1,0:T(8,128)(2,1)S(1)}, u32[]{:S(2)}, u32[]{:S(2)}) %all-to-all-start.4) | async-done | bytes 131104 | tf_op jit(solution)/shard_map/all_to_all | solution.py:189
  174.6 0.6 shard_map.120
  (7 shorter events, 0.2 us)
Async XLA Ops:
  3.9 13.6 %copy-start.7 = (bf16[4,128,128]{2,1,0:T(8,128)(2,1)S(1)}, bf16[4,128,128]{2,1,0:T(8,128)(2,1)}, u32[]{:S(2)}) copy-start(bf16[4,128,128]{2,1,0:T(8,128)(2,1)} %bwd_ref.2) | copy-start | bytes 393220
  3.9 13.6 %copy-start.8 = (bf16[4,128,128]{2,1,0:T(8,128)(2,1)S(1)}, bf16[4,128,128]{2,1,0:T(8,128)(2,1)}, u32[]{:S(2)}) copy-start(bf16[4,128,128]{2,1,0:T(8,128)(2,1)} %fwd_ref.2) | copy-start | bytes 393220
  3.9 42.5 %all-to-all-start = ((bf16[32,32,512]{2,1,0:T(8,128)(2,1)}), bf16[32,32,512]{2,1,0:T(8,128)(2,1)S(1)}, u32[]{:S(2)}, u32[]{:S(2)}) async-start(bf16[32,32,512]{2,1,0:T(8,128)(2,1)} %shard_map.109), calls=%async_computation | async-start | bytes 2097152 | tf_op jit(solution)/shard_map/all_to_all | solution.py:189
  46.4 1.7 copy-start
  48.1 5.1 %copy-start.6 = (bf16[4,128,128]{2,1,0:T(8,128)(2,1)S(1)}, bf16[4,128,128]{2,1,0:T(8,128)(2,1)}, u32[]{:S(2)}) copy-start(bf16[4,128,128]{2,1,0:T(8,128)(2,1)} %bwd_ref.1) | copy-start | bytes 393220
  48.1 34.0 %all-to-all-start.1 = ((bf16[32,32,512]{2,1,0:T(8,128)(2,1)}), bf16[32,32,512]{2,1,0:T(8,128)(2,1)S(1)}, u32[]{:S(2)}, u32[]{:S(2)}) async-start(bf16[32,32,512]{2,1,0:T(8,128)(2,1)} %shard_map.111), calls=%async_computation.1 | async-start | bytes 2097152 | tf_op jit(solution)/shard_map/all_to_all | solution.py:189
  82.1 1.9 %copy-start.2 = (bf16[32,32,512]{2,1,0:T(8,128)(2,1)}, bf16[32,32,512]{2,1,0:T(8,128)(2,1)S(1)}, u32[]{:S(2)}) copy-start(bf16[32,32,512]{2,1,0:T(8,128)(2,1)S(1)} %all-to-all-done.1.got_ref.got_hbm) | copy-start | bytes 3145732
  84.0 33.9 %all-to-all-start.2 = ((bf16[32,32,512]{2,1,0:T(8,128)(2,1)}), bf16[32,32,512]{2,1,0:T(8,128)(2,1)S(1)}, u32[]{:S(2)}, u32[]{:S(2)}) async-start(bf16[32,32,512]{2,1,0:T(8,128)(2,1)} %get-tuple-element.38), calls=%async_computation.2 | async-start | bytes 2097152 | tf_op jit(solution)/shard_map/all_to_all | solution.py:189
  91.2 10.3 %collective-permute-start = (bf16[4,4,8,128]{3,2,1,0:T(8,128)(2,1)S(1)}, bf16[4,4,8,128]{3,2,1,0:T(8,128)(2,1)S(1)}, u32[]{:S(2)}, u32[]{:S(2)}) collective-permute-start(bf16[4,4,8,128]{3,2,1,0:T(8,128)(2,1)S(1)} %get-tuple-element.57), channel_id=1, source_target_pairs={{0,256},{32,288},{64,320},{96,352},{128,384},{160,416},{192,448},{... | collective-permute-start | bytes 98312 | tf_op jit(solution)/shard_map/ppermute | solution.py:193
  94.3 7.3 %collective-permute-start.2 = (bf16[4,4,8,128]{3,2,1,0:T(8,128)(2,1)S(1)}, bf16[4,4,8,128]{3,2,1,0:T(8,128)(2,1)S(1)}, u32[]{:S(2)}, u32[]{:S(2)}) collective-permute-start(bf16[4,4,8,128]{3,2,1,0:T(8,128)(2,1)S(1)} %get-tuple-element.58), channel_id=1, source_target_pairs={{0,288},{32,256},{64,352},{96,320},{128,416},{160,384},{192,480},{... | collective-permute-start | bytes 98312 | tf_op jit(solution)/shard_map/ppermute | solution.py:193
  98.1 5.8 %collective-permute-start.1 = (bf16[4,4,8,128]{3,2,1,0:T(8,128)(2,1)S(1)}, bf16[4,4,8,128]{3,2,1,0:T(8,128)(2,1)S(1)}, u32[]{:S(2)}, u32[]{:S(2)}) collective-permute-start(bf16[4,4,8,128]{3,2,1,0:T(8,128)(2,1)S(1)} %get-tuple-element.59), channel_id=1, source_target_pairs={{0,32},{32,0},{64,96},{96,64},{128,160},{160,128},{192,224},{224,1... | collective-permute-start | bytes 98312 | tf_op jit(solution)/shard_map/ppermute | solution.py:193
  117.9 1.7 copy-start.1
  119.6 40.3 %all-to-all-start.3 = ((bf16[32,32,512]{2,1,0:T(8,128)(2,1)}), bf16[32,32,512]{2,1,0:T(8,128)(2,1)S(1)}, u32[]{:S(2)}, u32[]{:S(2)}) async-start(bf16[32,32,512]{2,1,0:T(8,128)(2,1)} %shard_map.116), calls=%async_computation.3 | async-start | bytes 2097152 | tf_op jit(solution)/shard_map/all_to_all | solution.py:189
  127.8 10.5 %collective-permute-start.3 = (bf16[4,8,8,128]{3,2,1,0:T(8,128)(2,1)S(1)}, bf16[4,8,8,128]{3,2,1,0:T(8,128)(2,1)S(1)}, u32[]{:S(2)}, u32[]{:S(2)}) collective-permute-start(bf16[4,8,8,128]{3,2,1,0:T(8,128)(2,1)S(1)} %get-tuple-element.54), channel_id=1, source_target_pairs={{0,256},{32,288},{64,320},{96,352},{128,384},{160,416},{192,448},{... | collective-permute-start | bytes 196616 | tf_op jit(solution)/shard_map/ppermute | solution.py:193
  130.9 7.4 %collective-permute-start.5 = (bf16[4,8,8,128]{3,2,1,0:T(8,128)(2,1)S(1)}, bf16[4,8,8,128]{3,2,1,0:T(8,128)(2,1)S(1)}, u32[]{:S(2)}, u32[]{:S(2)}) collective-permute-start(bf16[4,8,8,128]{3,2,1,0:T(8,128)(2,1)S(1)} %get-tuple-element.55), channel_id=1, source_target_pairs={{0,288},{32,256},{64,352},{96,320},{128,416},{160,384},{192,480},{... | collective-permute-start | bytes 196616 | tf_op jit(solution)/shard_map/ppermute | solution.py:193
  134.7 6.2 %collective-permute-start.4 = (bf16[4,8,8,128]{3,2,1,0:T(8,128)(2,1)S(1)}, bf16[4,8,8,128]{3,2,1,0:T(8,128)(2,1)S(1)}, u32[]{:S(2)}, u32[]{:S(2)}) collective-permute-start(bf16[4,8,8,128]{3,2,1,0:T(8,128)(2,1)S(1)} %get-tuple-element.56), channel_id=1, source_target_pairs={{0,32},{32,0},{64,96},{96,64},{128,160},{160,128},{192,224},{224,1... | collective-permute-start | bytes 196616 | tf_op jit(solution)/shard_map/ppermute | solution.py:193
  140.9 12.3 %collective-permute-start.6 = (bf16[12,8,128]{2,1,0:T(8,128)(2,1)S(1)}, bf16[12,8,128]{2,1,0:T(8,128)(2,1)S(1)}, u32[]{:S(2)}, u32[]{:S(2)}) collective-permute-start(bf16[12,8,128]{2,1,0:T(8,128)(2,1)S(1)} %get-tuple-element.60), channel_id=1, source_target_pairs={{0,64},{32,96},{64,0},{96,32},{128,192},{160,224},{192,128},{224,1... | collective-permute-start | bytes 73736 | tf_op jit(solution)/shard_map/ppermute | solution.py:193
  145.4 7.8 %collective-permute-start.8 = (bf16[12,8,128]{2,1,0:T(8,128)(2,1)S(1)}, bf16[12,8,128]{2,1,0:T(8,128)(2,1)S(1)}, u32[]{:S(2)}, u32[]{:S(2)}) collective-permute-start(bf16[12,8,128]{2,1,0:T(8,128)(2,1)S(1)} %get-tuple-element.61), channel_id=1, source_target_pairs={{0,192},{32,224},{64,128},{96,160},{128,64},{160,96},{192,0},{224,... | collective-permute-start | bytes 73736 | tf_op jit(solution)/shard_map/ppermute | solution.py:193
  150.2 9.6 %collective-permute-start.7 = (bf16[12,8,128]{2,1,0:T(8,128)(2,1)S(1)}, bf16[12,8,128]{2,1,0:T(8,128)(2,1)S(1)}, u32[]{:S(2)}, u32[]{:S(2)}) collective-permute-start(bf16[12,8,128]{2,1,0:T(8,128)(2,1)S(1)} %get-tuple-element.62), channel_id=1, source_target_pairs={{0,128},{32,160},{64,192},{96,224},{128,0},{160,32},{192,64},{224,... | collective-permute-start | bytes 73736 | tf_op jit(solution)/shard_map/ppermute | solution.py:193
  159.9 6.1 %copy-start.3 = (bf16[512,4,128]{2,1,0:T(4,128)(2,1)S(1)}, bf16[512,4,128]{2,1,0:T(4,128)(2,1)}, u32[]{:S(2)}) copy-start(bf16[512,4,128]{2,1,0:T(4,128)(2,1)} %param.6) | copy-start | bytes 1572868
  159.9 6.1 %copy-start.4 = (bf16[512,4,128]{2,1,0:T(4,128)(2,1)S(1)}, bf16[512,4,128]{2,1,0:T(4,128)(2,1)}, u32[]{:S(2)}) copy-start(bf16[512,4,128]{2,1,0:T(4,128)(2,1)} %param.11) | copy-start | bytes 1572868
  162.2 3.8 %copy-start.5 = (bf16[4,128,128]{2,1,0:T(8,128)(2,1)S(1)}, bf16[4,128,128]{2,1,0:T(8,128)(2,1)}, u32[]{:S(2)}) copy-start(bf16[4,128,128]{2,1,0:T(8,128)(2,1)} %r1_ref.1) | copy-start | bytes 393220
  162.2 12.4 %all-to-all-start.4 = ((bf16[16,4,8,128]{3,2,1,0:T(8,128)(2,1)}), bf16[16,4,8,128]{3,2,1,0:T(8,128)(2,1)S(1)}, u32[]{:S(2)}, u32[]{:S(2)}) async-start(bf16[16,4,8,128]{3,2,1,0:T(8,128)(2,1)} %shard_map.119), calls=%async_computation.4 | async-start | bytes 262144 | tf_op jit(solution)/shard_map/all_to_all | solution.py:189

commit v5 on v4

--- a/solution.py
+++ b/solution.py
@@ -52,8 +52,21 @@
     return dot(a, b, ((0,), (0,)))
 
 
-def put_rows(ref, first, value):
-    ref[:, first : first + 16, :] = value.astype(BF).reshape(32, 16, 512)
+def push(out_hbm, buf_ref, sems, first, rows_of):
+    copies = []
+    for half in range(2):
+        at = (pl.ds(16 * half, 16), pl.ds(first, 16))
+        value = rows_of(slice(256 * half, 256 * half + 256))
+        buf_ref[at] = value.astype(BF).reshape(16, 16, 512)
+        sem = sems.at[first // 8 + half]
+        copies.append(pltpu.make_async_copy(buf_ref.at[at], out_hbm.at[at], sem))
+        copies[-1].start()
+    return copies
+
+
+def finish(copies):
+    for copy in copies:
+        copy.wait()
 
 
 def get_rows(ref, first):
@@ -77,17 +90,21 @@
     return copies
 
 
-def first_kernel(x_hbm, g_hbm, r1_hbm, out_ref, xs_ref, gs_ref, x_ref, g_ref, r1_ref, sems):
+def first_kernel(
+    x_hbm, g_hbm, r1_hbm, out_hbm, xs_ref, gs_ref, x_ref, g_ref, r1_ref, sems, buf_ref, out_sems
+):
     r1_in, x_in, g_in = fetch(((r1_hbm, r1_ref), (x_hbm, x_ref), (g_hbm, g_ref)), sems)
     order = one_hot(in_to_flat)
     r1_in.wait()
     wide = right_one_out(r1_ref)
     x_in.wait()
     xs_ref[...] = x_ref[...].astype(F32)
-    put_rows(out_ref, 0, nt(wide, jnp.concatenate(by_block(xs_ref), axis=1)))
+    x = jnp.concatenate(by_block(xs_ref), axis=1)
+    fwd = push(out_hbm, buf_ref, out_sems, 0, lambda at: nt(wide[at], x))
     g_in.wait()
     gs_ref[...] = g_ref[...].astype(F32)
-    put_rows(out_ref, 16, nt(order, jnp.concatenate(by_block(gs_ref), axis=1)))
+    g = jnp.concatenate(by_block(gs_ref), axis=1)
+    finish(fwd + push(out_hbm, buf_ref, out_sems, 16, lambda at: nt(order[at], g)))
 
 
 def widen(w_ref, spread_in):
@@ -102,19 +119,23 @@
     bwd_out[...] = nt(widen(bwd_ref, spread_in), spread_out).astype(BF)
 
 
-def mix_kernel(got_ref, fwd_ref, bwd_ref, out_ref):
-    put_rows(out_ref, 0, nn(fwd_ref[...], get_rows(got_ref, 0)))
-    put_rows(out_ref, 16, nn(bwd_ref[...], get_rows(got_ref, 16)))
-
-
-def gelu_kernel(got_ref, fwd_ref, bwd_ref, out_ref, h_ref):
+def mix_kernel(got_ref, fwd_ref, bwd_ref, out_hbm, buf_ref, sems):
+    v = get_rows(got_ref, 0)
+    fwd = push(out_hbm, buf_ref, sems, 0, lambda at: nn(fwd_ref[at], v))
+    g = get_rows(got_ref, 16)
+    finish(fwd + push(out_hbm, buf_ref, sems, 16, lambda at: nn(bwd_ref[at], g)))
+
+
+def gelu_kernel(got_ref, fwd_ref, bwd_ref, out_hbm, h_ref, buf_ref, sems):
     z = get_rows(got_ref, 0).astype(F32)
     cdf = 0.5 * (1.0 + lax.erf(z * (1.0 / math.sqrt(2.0))))
     h = (z * cdf).astype(BF)
     h_ref[...] = h
-    put_rows(out_ref, 0, nn(fwd_ref[...], h))
+    fwd = push(out_hbm, buf_ref, sems, 0, lambda at: nn(fwd_ref[at], h))
     slope = cdf + z * jnp.exp(-0.5 * z * z) * (1.0 / math.sqrt(2.0 * math.pi))
-    put_rows(out_ref, 16, nn(bwd_ref[...], get_rows(got_ref, 16)) * slope)
+    g = get_rows(got_ref, 16)
+    bwd = push(out_hbm, buf_ref, sems, 16, lambda at: nn(bwd_ref[at], g) * slope[at])
+    finish(fwd + bwd)
 
 
 def grad_of(fwd, bwd, out_ref, first):
@@ -138,13 +159,23 @@
     grad_of(get_rows(three_ref, 0), get_rows(one_ref, 16), out_ref, 4)
 
 
-def right_grad_kernel(got_ref, x_hbm, out_ref, xs_ref, x_ref, sems):
+def turn_kernel(x_hbm, out_hbm, xs_ref, x_ref, xt_ref, sems):
     (x_in,) = fetch(((x_hbm, x_ref),), sems)
-    d = nn(one_hot(flat_to_out), get_rows(got_ref, 16)).astype(BF)
     x_in.wait()
     xs_ref[...] = x_ref[...].astype(F32)
-    for b, x in enumerate(by_block(xs_ref)):
-        g = jnp.transpose(nn(d[128 * b : 128 * b + 128], x))
+    for b in range(4):
+        xt_ref[b] = jnp.transpose(xs_ref[pl.ds(b, 512, stride=4), :]).astype(BF)
+    out = pltpu.make_async_copy(xt_ref, out_hbm, sems.at[1])
+    out.start()
+    out.wait()
+
+
+def right_grad_kernel(got_ref, xt_hbm, out_ref, xt_ref, sems):
+    (xt_in,) = fetch(((xt_hbm, xt_ref),), sems)
+    d = nn(one_hot(flat_to_out), get_rows(got_ref, 16)).astype(BF)
+    xt_in.wait()
+    for b in range(4):
+        g = nt(xt_ref[b], d[128 * b : 128 * b + 128])
         out_ref[:, b, :, :] = g.reshape(16, 8, 128).astype(BF)
 
 
@@ -170,15 +201,18 @@
 WIDE_ROWS = pltpu.VMEM(ROWS, F32)
 HALF_ROWS = pltpu.VMEM(ROWS, BF)
 CHUNK = pltpu.VMEM((32, 32, 512), BF)
-
-
-def call(kernel, shapes, *args, scratch=(), far=()):
+XT = pltpu.VMEM((4, 128, 512), BF)
+
+
+def call(kernel, shapes, *args, scratch=(), far=(), far_out=()):
     args = [pltpu.with_memory_space_constraint(a, pltpu.HBM) if n in far else a for n, a in enumerate(args)]
     outs = [jax.ShapeDtypeStruct(s, d) for s, d in shapes]
     specs = [pl.BlockSpec(memory_space=pltpu.HBM if n in far else pltpu.VMEM) for n in range(len(args))]
+    out_specs = [pl.BlockSpec(memory_space=pltpu.HBM if n in far_out else pltpu.VMEM) for n in range(len(outs))]
     return pl.pallas_call(
         kernel,
         out_shape=outs,
+        out_specs=out_specs,
         in_specs=specs,
         scratch_shapes=scratch,
         compiler_params=pltpu.CompilerParams(vmem_limit_bytes=16 << 20),
@@ -219,7 +253,7 @@
         )
 
     half = total.astype(BF)
-    own = of(total, me)
+    own = lax.optimization_barrier(of(total, me))
     for mask in (2, 4, 6):
         own = own + sent(of(half, me ^ mask), mask).astype(F32)
     return own
@@ -234,6 +268,7 @@
     g = out_grad.reshape(ROWS)
     chunk = ((32, 32, 512), BF)
     square = ((512, 512), BF)
+    pushed = dict(scratch=(CHUNK, pltpu.SemaphoreType.DMA((4,))), far_out=(0,))
     (send,) = call(
         first_kernel,
         [chunk],
@@ -247,16 +282,28 @@
             HALF_ROWS,
             pltpu.VMEM((4, 128, 128), BF),
             pltpu.SemaphoreType.DMA((3,)),
+            CHUNK,
+            pltpu.SemaphoreType.DMA((4,)),
         ),
         far=(0, 1, 2),
+        far_out=(0,),
     )
     one = swap(send, "tensor")
     fwd, bwd = call(weights_kernel, [square] * 2, *after(send, left_one, left_two))
-    (send,) = call(mix_kernel, [chunk], one, fwd, bwd)
+    (send,) = call(mix_kernel, [chunk], one, fwd, bwd, **pushed)
     (one,) = after(send, one)
     two = swap(send, "tensor")
     fwd, bwd = call(weights_kernel, [square] * 2, *after(send, right_two, right_two))
-    send, h = call(gelu_kernel, [chunk, square], two, fwd, bwd)
+    (xt,) = call(
+        turn_kernel,
+        [((4, 128, 512), BF)],
+        *after(send, x),
+        scratch=(WIDE_ROWS, HALF_ROWS, XT, pltpu.SemaphoreType.DMA((2,))),
+        far=(0,),
+        far_out=(0,),
+    )
+    two, xt = lax.optimization_barrier((two, xt))
+    send, h = call(gelu_kernel, [chunk, square], two, fwd, bwd, **pushed)
     h, two = after(send, h, two)
     three = swap(send, "tensor")
     fwd, bwd = call(weights_kernel, [square] * 2, *after(send, left_two, left_one))
@@ -270,7 +317,7 @@
     )
     gr2 = added_near(gr2)
     three, gr2 = lax.optimization_barrier((three, gr2))
-    (send,) = call(mix_kernel, [chunk], three, fwd, bwd)
+    (send,) = call(mix_kernel, [chunk], three, fwd, bwd, **pushed)
     (three,) = after(send, three)
     four = swap(send, "tensor")
     (left,) = call(
@@ -283,13 +330,12 @@
     )
     left = added_near(left)
     sums = added_far(jnp.concatenate((gr2, left), axis=1))
-    four, sums = lax.optimization_barrier((four, sums))
     (send,) = call(
         right_grad_kernel,
         [((16, 4, 8, 128), BF)],
         four,
-        x,
-        scratch=(WIDE_ROWS, HALF_ROWS, pltpu.SemaphoreType.DMA((1,))),
+        xt,
+        scratch=(XT, pltpu.SemaphoreType.DMA((1,))),
         far=(1,),
     )
     got = swap(send, "dp")

time: 176 us -> 173 us (0.983)
  waiting for transfers between devices: 88.5 us -> 79.8 us
  starting transfers between devices: 63.1 us -> 67.2 us
    ppermute x9, waiting for transfers between devices: 12.8 us -> 6.15 us  [sent(): return lax.ppermute(x, 'dp', [(i, i ^ mask) for i in range(16)])]
    all_to_all x5, starting transfers between devices: 32.5 us -> 36.6 us  [swap(): return lax.all_to_all(x, axis, 0, 0, tiled=True)]
    all_to_all x5, waiting for transfers between devices: 75.6 us -> 73.7 us  [swap(): return lax.all_to_all(x, axis, 0, 0, tiled=True)]
    pallas_call x12 -> x13, Pallas kernels: 21.9 us -> 22.3 us  [call(): pl.pallas_call(kernel, out_shape=outs, out_specs=out_specs, in_specs=spec...]
  transfers between devices with their start and end apart: 14 -> 14, of which waited for: 9 -> 8; matrix products, arithmetic and copies ran while one was open for 0% -> 0% of each run, Pallas kernels for 6% -> 8%
where the time goes in v5:
time: 173 us; the launch traced here: 172 us
  waiting for transfers between devices  79.8 us (46%)
  starting transfers between devices  67.2 us (39%)
  Pallas kernels  22.3 us (13%)
    all_to_all x5, waiting for transfers between devices, swap(): return lax.all_to_all(x, axis, 0, 0, tiled=True)  73.7 us
    all_to_all x5, starting transfers between devices, swap(): return lax.all_to_all(x, axis, 0, 0, tiled=True)  36.6 us
    ppermute x9, starting transfers between devices, sent(): return lax.ppermute(x, 'dp', [(i, i ^ mask) for i in range(16)])  30.6 us
    pallas_call x13, Pallas kernels, call(): pl.pallas_call(kernel, out_shape=outs, out_specs=out_specs, in_specs=spec...  22.3 us
    ppermute x9, waiting for transfers between devices, sent(): return lax.ppermute(x, 'dp', [(i, i ^ mask) for i in range(16)])  6.15 us
  transfers between devices with their start and end apart: 14, of which 8 were waited for; matrix products, arithmetic and copies ran while one was open for 0% of the time, Pallas kernels for 8%

profile of v5, /device:TPU:4, one launch (start us, length us, event | category | flops | bytes accessed | tf_op | source)
XLA Modules:
  0.0 172.0 jit_solution(17687764890019584110)
XLA Ops:
  0.6 3.1 %shard_map.109 = bf16[32,32,512]{2,1,0:T(8,128)(2,1)} custom-call(bf16[2048,128]{1,0:T(8,128)(2,1)} %bitcast.34, bf16[2048,128]{1,0:T(8,128)(2,1)} %bitcast.37, bf16[4,128,128]{2,1,0:T(8,128)(2,1)} %r1_ref.1), custom_call_target="tpu_custom_call" | custom-call | tf_op jit(solution)/shard_map/pallas_call | solution.py:212
  3.7 0.0 copy-start.8
  3.7 0.0 copy-start.9
  3.7 13.6 %all-to-all-start = ((bf16[32,32,512]{2,1,0:T(8,128)(2,1)}), bf16[32,32,512]{2,1,0:T(8,128)(2,1)S(1)}, u32[]{:S(2)}, u32[]{:S(2)}) async-start(bf16[32,32,512]{2,1,0:T(8,128)(2,1)} %shard_map.109), calls=%async_computation | async-start | bytes 2097152 | tf_op jit(solution)/shard_map/all_to_all | solution.py:223
  17.3 0.0 copy-done.8
  17.3 0.0 copy-done.9
  17.3 1.1 shard_map.110
  18.4 27.8 %all-to-all-done.got_ref.one_hbm = bf16[32,32,512]{2,1,0:T(8,128)(2,1)S(1)} async-done(((bf16[32,32,512]{2,1,0:T(8,128)(2,1)}), bf16[32,32,512]{2,1,0:T(8,128)(2,1)S(1)}, u32[]{:S(2)}, u32[]{:S(2)}) %all-to-all-start) | async-done | bytes 1048608 | tf_op jit(solution)/shard_map/all_to_all | solution.py:223
  46.2 0.0 copy-start
  46.2 1.5 shard_map.111
  47.7 0.0 copy-done
  47.7 5.0 %all-to-all-start.1 = ((bf16[32,32,512]{2,1,0:T(8,128)(2,1)}), bf16[32,32,512]{2,1,0:T(8,128)(2,1)S(1)}, u32[]{:S(2)}, u32[]{:S(2)}) async-start(bf16[32,32,512]{2,1,0:T(8,128)(2,1)} %shard_map.111), calls=%async_computation.1 | async-start | bytes 2097152 | tf_op jit(solution)/shard_map/all_to_all | solution.py:223
  52.7 0.0 copy-start.7
  52.7 1.4 shard_map.112.xt_hbm
  54.1 0.0 copy-start.5
  54.1 0.8 copy-done.5
  54.9 0.0 copy-done.7
  54.9 1.1 shard_map.113
  56.0 25.6 %all-to-all-done.1.got_ref.got_hbm = bf16[32,32,512]{2,1,0:T(8,128)(2,1)S(1)} async-done(((bf16[32,32,512]{2,1,0:T(8,128)(2,1)}), bf16[32,32,512]{2,1,0:T(8,128)(2,1)S(1)}, u32[]{:S(2)}, u32[]{:S(2)}) %all-to-all-start.1) | async-done | bytes 1048608 | tf_op jit(solution)/shard_map/all_to_all | solution.py:223
  81.6 0.0 copy-start.2
  81.6 1.7 shard_map.114
  83.3 0.0 copy-done.2
  83.3 5.0 %all-to-all-start.2 = ((bf16[32,32,512]{2,1,0:T(8,128)(2,1)}), bf16[32,32,512]{2,1,0:T(8,128)(2,1)S(1)}, u32[]{:S(2)}, u32[]{:S(2)}) async-start(bf16[32,32,512]{2,1,0:T(8,128)(2,1)} %get-tuple-element.41), calls=%async_computation.2 | async-start | bytes 2097152 | tf_op jit(solution)/shard_map/all_to_all | solution.py:223
  88.3 2.1 %shard_map.115 = bf16[16,4,8,128]{3,2,1,0:T(8,128)(2,1)S(1)} custom-call(bf16[512,512]{1,0:T(8,128)(2,1)S(1)} %get-tuple-element.43.h_ref, bf16[32,32,512]{2,1,0:T(8,128)(2,1)} %copy-done.2), custom_call_target="tpu_custom_call" | custom-call | tf_op jit(solution)/shard_map/pallas_call | solution.py:212
  90.5 3.1 %collective-permute-start = (bf16[4,4,8,128]{3,2,1,0:T(8,128)(2,1)S(1)}, bf16[4,4,8,128]{3,2,1,0:T(8,128)(2,1)S(1)}, u32[]{:S(2)}, u32[]{:S(2)}) collective-permute-start(bf16[4,4,8,128]{3,2,1,0:T(8,128)(2,1)S(1)} %get-tuple-element.59), channel_id=1, source_target_pairs={{0,256},{32,288},{64,320},{96,352},{128,384},{160,416},{192,448},{... | collective-permute-start | bytes 98312 | tf_op jit(solution)/shard_map/ppermute | solution.py:227
  93.6 3.8 %collective-permute-start.2 = (bf16[4,4,8,128]{3,2,1,0:T(8,128)(2,1)S(1)}, bf16[4,4,8,128]{3,2,1,0:T(8,128)(2,1)S(1)}, u32[]{:S(2)}, u32[]{:S(2)}) collective-permute-start(bf16[4,4,8,128]{3,2,1,0:T(8,128)(2,1)S(1)} %get-tuple-element.60), channel_id=1, source_target_pairs={{0,288},{32,256},{64,352},{96,320},{128,416},{160,384},{192,480},{... | collective-permute-start | bytes 98312 | tf_op jit(solution)/shard_map/ppermute | solution.py:227
  97.4 2.3 %collective-permute-start.1 = (bf16[4,4,8,128]{3,2,1,0:T(8,128)(2,1)S(1)}, bf16[4,4,8,128]{3,2,1,0:T(8,128)(2,1)S(1)}, u32[]{:S(2)}, u32[]{:S(2)}) collective-permute-start(bf16[4,4,8,128]{3,2,1,0:T(8,128)(2,1)S(1)} %get-tuple-element.61), channel_id=1, source_target_pairs={{0,32},{32,0},{64,96},{96,64},{128,160},{160,128},{192,224},{224,1... | collective-permute-start | bytes 98312 | tf_op jit(solution)/shard_map/ppermute | solution.py:227
  99.7 1.1 shard_map.116
  100.8 0.0 collective-permute-done
  100.8 0.0 collective-permute-done.2
  100.9 2.3 %collective-permute-done.1 = bf16[4,4,8,128]{3,2,1,0:T(8,128)(2,1)S(1)} collective-permute-done((bf16[4,4,8,128]{3,2,1,0:T(8,128)(2,1)S(1)}, bf16[4,4,8,128]{3,2,1,0:T(8,128)(2,1)S(1)}, u32[]{:S(2)}, u32[]{:S(2)}) %collective-permute-start.1) | collective-permute-done | bytes 32800 | tf_op jit(solution)/shard_map/ppermute | solution.py:227
  103.2 14.0 %all-to-all-done.2.got_ref.three_hbm = bf16[32,32,512]{2,1,0:T(8,128)(2,1)S(1)} async-done(((bf16[32,32,512]{2,1,0:T(8,128)(2,1)}), bf16[32,32,512]{2,1,0:T(8,128)(2,1)S(1)}, u32[]{:S(2)}, u32[]{:S(2)}) %all-to-all-start.2) | async-done | bytes 1048608 | tf_op jit(solution)/shard_map/all_to_all | solution.py:223
  117.2 0.0 copy-start.1
  117.2 1.5 shard_map.117
  118.7 0.0 copy-done.1
  118.7 5.0 %all-to-all-start.3 = ((bf16[32,32,512]{2,1,0:T(8,128)(2,1)}), bf16[32,32,512]{2,1,0:T(8,128)(2,1)S(1)}, u32[]{:S(2)}, u32[]{:S(2)}) async-start(bf16[32,32,512]{2,1,0:T(8,128)(2,1)} %shard_map.117), calls=%async_computation.3 | async-start | bytes 2097152 | tf_op jit(solution)/shard_map/all_to_all | solution.py:223
  123.7 3.2 %shard_map.121 = bf16[16,8,8,128]{3,2,1,0:T(8,128)(2,1)S(1)} custom-call(bf16[32,32,512]{2,1,0:T(8,128)(2,1)} %copy-done, bf16[32,32,512]{2,1,0:T(8,128)(2,1)} %copy-done.1), custom_call_target="tpu_custom_call" | custom-call | tf_op jit(solution)/shard_map/pallas_call | solution.py:212
  126.9 3.1 %collective-permute-start.3 = (bf16[4,8,8,128]{3,2,1,0:T(8,128)(2,1)S(1)}, bf16[4,8,8,128]{3,2,1,0:T(8,128)(2,1)S(1)}, u32[]{:S(2)}, u32[]{:S(2)}) collective-permute-start(bf16[4,8,8,128]{3,2,1,0:T(8,128)(2,1)S(1)} %get-tuple-element.56), channel_id=1, source_target_pairs={{0,256},{32,288},{64,320},{96,352},{128,384},{160,416},{192,448},{... | collective-permute-start | bytes 196616 | tf_op jit(solution)/shard_map/ppermute | solution.py:227
  130.0 3.8 %collective-permute-start.5 = (bf16[4,8,8,128]{3,2,1,0:T(8,128)(2,1)S(1)}, bf16[4,8,8,128]{3,2,1,0:T(8,128)(2,1)S(1)}, u32[]{:S(2)}, u32[]{:S(2)}) collective-permute-start(bf16[4,8,8,128]{3,2,1,0:T(8,128)(2,1)S(1)} %get-tuple-element.57), channel_id=1, source_target_pairs={{0,288},{32,256},{64,352},{96,320},{128,416},{160,384},{192,480},{... | collective-permute-start | bytes 196616 | tf_op jit(solution)/shard_map/ppermute | solution.py:227
  133.8 2.4 %collective-permute-start.4 = (bf16[4,8,8,128]{3,2,1,0:T(8,128)(2,1)S(1)}, bf16[4,8,8,128]{3,2,1,0:T(8,128)(2,1)S(1)}, u32[]{:S(2)}, u32[]{:S(2)}) collective-permute-start(bf16[4,8,8,128]{3,2,1,0:T(8,128)(2,1)S(1)} %get-tuple-element.58), channel_id=1, source_target_pairs={{0,32},{32,0},{64,96},{96,64},{128,160},{160,128},{192,224},{224,1... | collective-permute-start | bytes 196616 | tf_op jit(solution)/shard_map/ppermute | solution.py:227
  136.1 1.3 collective-permute-done.3
  137.4 0.0 collective-permute-done.5
  137.4 2.5 %collective-permute-done.4 = bf16[4,8,8,128]{3,2,1,0:T(8,128)(2,1)S(1)} collective-permute-done((bf16[4,8,8,128]{3,2,1,0:T(8,128)(2,1)S(1)}, bf16[4,8,8,128]{3,2,1,0:T(8,128)(2,1)S(1)}, u32[]{:S(2)}, u32[]{:S(2)}) %collective-permute-start.4) | collective-permute-done | bytes 65568 | tf_op jit(solution)/shard_map/ppermute | solution.py:227
  140.0 4.5 %collective-permute-start.6 = (bf16[12,8,128]{2,1,0:T(8,128)(2,1)S(1)}, bf16[12,8,128]{2,1,0:T(8,128)(2,1)S(1)}, u32[]{:S(2)}, u32[]{:S(2)}) collective-permute-start(bf16[12,8,128]{2,1,0:T(8,128)(2,1)S(1)} %get-tuple-element.62), channel_id=1, source_target_pairs={{0,64},{32,96},{64,0},{96,32},{128,192},{160,224},{192,128},{224,1... | collective-permute-start | bytes 73736 | tf_op jit(solution)/shard_map/ppermute | solution.py:227
  144.5 4.8 %collective-permute-start.8 = (bf16[12,8,128]{2,1,0:T(8,128)(2,1)S(1)}, bf16[12,8,128]{2,1,0:T(8,128)(2,1)S(1)}, u32[]{:S(2)}, u32[]{:S(2)}) collective-permute-start(bf16[12,8,128]{2,1,0:T(8,128)(2,1)S(1)} %get-tuple-element.63), channel_id=1, source_target_pairs={{0,192},{32,224},{64,128},{96,160},{128,64},{160,96},{192,0},{224,... | collective-permute-start | bytes 73736 | tf_op jit(solution)/shard_map/ppermute | solution.py:227
  149.3 2.9 %collective-permute-start.7 = (bf16[12,8,128]{2,1,0:T(8,128)(2,1)S(1)}, bf16[12,8,128]{2,1,0:T(8,128)(2,1)S(1)}, u32[]{:S(2)}, u32[]{:S(2)}) collective-permute-start(bf16[12,8,128]{2,1,0:T(8,128)(2,1)S(1)} %get-tuple-element.64), channel_id=1, source_target_pairs={{0,128},{32,160},{64,192},{96,224},{128,0},{160,32},{192,64},{224,... | collective-permute-start | bytes 73736 | tf_op jit(solution)/shard_map/ppermute | solution.py:227
  152.3 0.3 all-to-all-done.3.got_ref
  152.6 0.0 copy-start.4
  152.6 0.0 copy-start.6
  152.6 2.2 %shard_map.119 = bf16[16,4,8,128]{3,2,1,0:T(8,128)(2,1)} custom-call(bf16[32,32,512]{2,1,0:T(8,128)(2,1)S(1)} %all-to-all-done.3.got_ref, bf16[4,128,512]{2,1,0:T(8,128)(2,1)} %copy-done.5), custom_call_target="tpu_custom_call" | custom-call | tf_op jit(solution)/shard_map/pallas_call | solution.py:212
  154.7 0.0 copy-start.3
  154.8 8.0 %all-to-all-start.4 = ((bf16[16,4,8,128]{3,2,1,0:T(8,128)(2,1)}), bf16[16,4,8,128]{3,2,1,0:T(8,128)(2,1)S(1)}, u32[]{:S(2)}, u32[]{:S(2)}) async-start(bf16[16,4,8,128]{3,2,1,0:T(8,128)(2,1)} %shard_map.119), calls=%async_computation.4 | async-start | bytes 262144 | tf_op jit(solution)/shard_map/all_to_all | solution.py:223
  162.8 0.0 collective-permute-done.6
  162.8 0.0 collective-permute-done.8
  162.8 0.0 collective-permute-done.7
  162.8 0.6 fusion.7
  163.4 0.0 copy-done.4
  163.4 0.0 copy-done.6
  163.4 0.0 copy-done.3
  163.4 1.9 %shard_map.118 = (bf16[2048,128]{1,0:T(8,128)(2,1)}, bf16[2048,128]{1,0:T(8,128)(2,1)}) custom-call(bf16[32,32,512]{2,1,0:T(8,128)(2,1)S(1)} %all-to-all-done.3.got_ref, bf16[2048,128]{1,0:T(8,128)(2,1)S(1)} %bitcast.36, bf16[2048,128]{1,0:T(8,128)(2,1)S(1)} %bitcast.38, bf16[4,128,128]{2,1,0:T(8,128)(2,1)S(1)} %copy-done.6), custom_call_target="tpu_custom_call" | custom-call | tf_op jit(solution)/shard_map/pallas_call | solution.py:212
  165.4 6.0 %all-to-all-done.4.got_ref = bf16[16,4,8,128]{3,2,1,0:T(8,128)(2,1)S(1)} async-done(((bf16[16,4,8,128]{3,2,1,0:T(8,128)(2,1)}), bf16[16,4,8,128]{3,2,1,0:T(8,128)(2,1)S(1)}, u32[]{:S(2)}, u32[]{:S(2)}) %all-to-all-start.4) | async-done | bytes 131104 | tf_op jit(solution)/shard_map/all_to_all | solution.py:223
  171.3 0.6 shard_map.120
  (8 shorter events, 0.2 us)
Async XLA Ops:
  3.7 13.6 %copy-start.8 = (bf16[4,128,128]{2,1,0:T(8,128)(2,1)S(1)}, bf16[4,128,128]{2,1,0:T(8,128)(2,1)}, u32[]{:S(2)}) copy-start(bf16[4,128,128]{2,1,0:T(8,128)(2,1)} %bwd_ref.2) | copy-start | bytes 393220
  3.7 13.6 %copy-start.9 = (bf16[4,128,128]{2,1,0:T(8,128)(2,1)S(1)}, bf16[4,128,128]{2,1,0:T(8,128)(2,1)}, u32[]{:S(2)}) copy-start(bf16[4,128,128]{2,1,0:T(8,128)(2,1)} %fwd_ref.2) | copy-start | bytes 393220
  3.7 42.5 %all-to-all-start = ((bf16[32,32,512]{2,1,0:T(8,128)(2,1)}), bf16[32,32,512]{2,1,0:T(8,128)(2,1)S(1)}, u32[]{:S(2)}, u32[]{:S(2)}) async-start(bf16[32,32,512]{2,1,0:T(8,128)(2,1)} %shard_map.109), calls=%async_computation | async-start | bytes 2097152 | tf_op jit(solution)/shard_map/all_to_all | solution.py:223
  46.2 1.5 copy-start
  47.7 33.9 %all-to-all-start.1 = ((bf16[32,32,512]{2,1,0:T(8,128)(2,1)}), bf16[32,32,512]{2,1,0:T(8,128)(2,1)S(1)}, u32[]{:S(2)}, u32[]{:S(2)}) async-start(bf16[32,32,512]{2,1,0:T(8,128)(2,1)} %shard_map.111), calls=%async_computation.1 | async-start | bytes 2097152 | tf_op jit(solution)/shard_map/all_to_all | solution.py:223
  52.7 2.2 %copy-start.7 = (bf16[4,128,128]{2,1,0:T(8,128)(2,1)S(1)}, bf16[4,128,128]{2,1,0:T(8,128)(2,1)}, u32[]{:S(2)}) copy-start(bf16[4,128,128]{2,1,0:T(8,128)(2,1)} %bwd_ref.1) | copy-start | bytes 393220
  54.1 0.8 copy-start.5
  81.6 1.7 copy-start.2
  83.3 33.9 %all-to-all-start.2 = ((bf16[32,32,512]{2,1,0:T(8,128)(2,1)}), bf16[32,32,512]{2,1,0:T(8,128)(2,1)S(1)}, u32[]{:S(2)}, u32[]{:S(2)}) async-start(bf16[32,32,512]{2,1,0:T(8,128)(2,1)} %get-tuple-element.41), calls=%async_computation.2 | async-start | bytes 2097152 | tf_op jit(solution)/shard_map/all_to_all | solution.py:223
  90.5 10.3 %collective-permute-start = (bf16[4,4,8,128]{3,2,1,0:T(8,128)(2,1)S(1)}, bf16[4,4,8,128]{3,2,1,0:T(8,128)(2,1)S(1)}, u32[]{:S(2)}, u32[]{:S(2)}) collective-permute-start(bf16[4,4,8,128]{3,2,1,0:T(8,128)(2,1)S(1)} %get-tuple-element.59), channel_id=1, source_target_pairs={{0,256},{32,288},{64,320},{96,352},{128,384},{160,416},{192,448},{... | collective-permute-start | bytes 98312 | tf_op jit(solution)/shard_map/ppermute | solution.py:227
  93.6 7.3 %collective-permute-start.2 = (bf16[4,4,8,128]{3,2,1,0:T(8,128)(2,1)S(1)}, bf16[4,4,8,128]{3,2,1,0:T(8,128)(2,1)S(1)}, u32[]{:S(2)}, u32[]{:S(2)}) collective-permute-start(bf16[4,4,8,128]{3,2,1,0:T(8,128)(2,1)S(1)} %get-tuple-element.60), channel_id=1, source_target_pairs={{0,288},{32,256},{64,352},{96,320},{128,416},{160,384},{192,480},{... | collective-permute-start | bytes 98312 | tf_op jit(solution)/shard_map/ppermute | solution.py:227
  97.4 5.8 %collective-permute-start.1 = (bf16[4,4,8,128]{3,2,1,0:T(8,128)(2,1)S(1)}, bf16[4,4,8,128]{3,2,1,0:T(8,128)(2,1)S(1)}, u32[]{:S(2)}, u32[]{:S(2)}) collective-permute-start(bf16[4,4,8,128]{3,2,1,0:T(8,128)(2,1)S(1)} %get-tuple-element.61), channel_id=1, source_target_pairs={{0,32},{32,0},{64,96},{96,64},{128,160},{160,128},{192,224},{224,1... | collective-permute-start | bytes 98312 | tf_op jit(solution)/shard_map/ppermute | solution.py:227
  117.2 1.5 copy-start.1
  118.7 33.9 %all-to-all-start.3 = ((bf16[32,32,512]{2,1,0:T(8,128)(2,1)}), bf16[32,32,512]{2,1,0:T(8,128)(2,1)S(1)}, u32[]{:S(2)}, u32[]{:S(2)}) async-start(bf16[32,32,512]{2,1,0:T(8,128)(2,1)} %shard_map.117), calls=%async_computation.3 | async-start | bytes 2097152 | tf_op jit(solution)/shard_map/all_to_all | solution.py:223
  126.9 10.5 %collective-permute-start.3 = (bf16[4,8,8,128]{3,2,1,0:T(8,128)(2,1)S(1)}, bf16[4,8,8,128]{3,2,1,0:T(8,128)(2,1)S(1)}, u32[]{:S(2)}, u32[]{:S(2)}) collective-permute-start(bf16[4,8,8,128]{3,2,1,0:T(8,128)(2,1)S(1)} %get-tuple-element.56), channel_id=1, source_target_pairs={{0,256},{32,288},{64,320},{96,352},{128,384},{160,416},{192,448},{... | collective-permute-start | bytes 196616 | tf_op jit(solution)/shard_map/ppermute | solution.py:227
  130.0 7.4 %collective-permute-start.5 = (bf16[4,8,8,128]{3,2,1,0:T(8,128)(2,1)S(1)}, bf16[4,8,8,128]{3,2,1,0:T(8,128)(2,1)S(1)}, u32[]{:S(2)}, u32[]{:S(2)}) collective-permute-start(bf16[4,8,8,128]{3,2,1,0:T(8,128)(2,1)S(1)} %get-tuple-element.57), channel_id=1, source_target_pairs={{0,288},{32,256},{64,352},{96,320},{128,416},{160,384},{192,480},{... | collective-permute-start | bytes 196616 | tf_op jit(solution)/shard_map/ppermute | solution.py:227
  133.8 6.2 %collective-permute-start.4 = (bf16[4,8,8,128]{3,2,1,0:T(8,128)(2,1)S(1)}, bf16[4,8,8,128]{3,2,1,0:T(8,128)(2,1)S(1)}, u32[]{:S(2)}, u32[]{:S(2)}) collective-permute-start(bf16[4,8,8,128]{3,2,1,0:T(8,128)(2,1)S(1)} %get-tuple-element.58), channel_id=1, source_target_pairs={{0,32},{32,0},{64,96},{96,64},{128,160},{160,128},{192,224},{224,1... | collective-permute-start | bytes 196616 | tf_op jit(solution)/shard_map/ppermute | solution.py:227
  140.0 22.8 %collective-permute-start.6 = (bf16[12,8,128]{2,1,0:T(8,128)(2,1)S(1)}, bf16[12,8,128]{2,1,0:T(8,128)(2,1)S(1)}, u32[]{:S(2)}, u32[]{:S(2)}) collective-permute-start(bf16[12,8,128]{2,1,0:T(8,128)(2,1)S(1)} %get-tuple-element.62), channel_id=1, source_target_pairs={{0,64},{32,96},{64,0},{96,32},{128,192},{160,224},{192,128},{224,1... | collective-permute-start | bytes 73736 | tf_op jit(solution)/shard_map/ppermute | solution.py:227
  144.5 18.3 %collective-permute-start.8 = (bf16[12,8,128]{2,1,0:T(8,128)(2,1)S(1)}, bf16[12,8,128]{2,1,0:T(8,128)(2,1)S(1)}, u32[]{:S(2)}, u32[]{:S(2)}) collective-permute-start(bf16[12,8,128]{2,1,0:T(8,128)(2,1)S(1)} %get-tuple-element.63), channel_id=1, source_target_pairs={{0,192},{32,224},{64,128},{96,160},{128,64},{160,96},{192,0},{224,... | collective-permute-start | bytes 73736 | tf_op jit(solution)/shard_map/ppermute | solution.py:227
  149.3 13.5 %collective-permute-start.7 = (bf16[12,8,128]{2,1,0:T(8,128)(2,1)S(1)}, bf16[12,8,128]{2,1,0:T(8,128)(2,1)S(1)}, u32[]{:S(2)}, u32[]{:S(2)}) collective-permute-start(bf16[12,8,128]{2,1,0:T(8,128)(2,1)S(1)} %get-tuple-element.64), channel_id=1, source_target_pairs={{0,128},{32,160},{64,192},{96,224},{128,0},{160,32},{192,64},{224,... | collective-permute-start | bytes 73736 | tf_op jit(solution)/shard_map/ppermute | solution.py:227
  152.6 10.9 %copy-start.4 = (bf16[512,4,128]{2,1,0:T(4,128)(2,1)S(1)}, bf16[512,4,128]{2,1,0:T(4,128)(2,1)}, u32[]{:S(2)}) copy-start(bf16[512,4,128]{2,1,0:T(4,128)(2,1)} %param.11) | copy-start | bytes 1572868
  152.6 10.9 %copy-start.6 = (bf16[4,128,128]{2,1,0:T(8,128)(2,1)S(1)}, bf16[4,128,128]{2,1,0:T(8,128)(2,1)}, u32[]{:S(2)}) copy-start(bf16[4,128,128]{2,1,0:T(8,128)(2,1)} %r1_ref.1) | copy-start | bytes 393220
  154.7 8.7 %copy-start.3 = (bf16[512,4,128]{2,1,0:T(4,128)(2,1)S(1)}, bf16[512,4,128]{2,1,0:T(4,128)(2,1)}, u32[]{:S(2)}) copy-start(bf16[512,4,128]{2,1,0:T(4,128)(2,1)} %param.6) | copy-start | bytes 1572868
  154.8 16.6 %all-to-all-start.4 = ((bf16[16,4,8,128]{3,2,1,0:T(8,128)(2,1)}), bf16[16,4,8,128]{3,2,1,0:T(8,128)(2,1)S(1)}, u32[]{:S(2)}, u32[]{:S(2)}) async-start(bf16[16,4,8,128]{3,2,1,0:T(8,128)(2,1)} %shard_map.119), calls=%async_computation.4 | async-start | bytes 262144 | tf_op jit(solution)/shard_map/all_to_all | solution.py:223
